TPU v7x, 32 devices: a whole 2x2x4 slice. The times are simulated.
32 devices in a mesh: seq: 8 (over z, y), head: 4 (over x, core).
Axes of the slice: x: 2, y: 2, z: 4, core: 2. Of those that a mesh axis runs over, the one named last changes fastest.
Arguments:
- tokens: bfloat16 [8192, 2048], P('seq'), may hold values from -6 to 6
- w_query: bfloat16 [2048, 2048], P(None, 'head'), may hold values from -0.125 to 0.125
- w_key: bfloat16 [2048, 2048], P(None, 'head'), may hold values from -0.125 to 0.125
- w_value: bfloat16 [2048, 2048], P(None, 'head'), may hold values from -0.125 to 0.125
- w_out: bfloat16 [2048, 2048], P('head'), may hold values from -0.125 to 0.125
- norm_gain: float32 [2048], P('head'), may hold values from 0.5 to 1.5
- forget_rate: float32 [8192, 16], P('seq', 'head'), may hold values from 0 to 2, as said below
- routing: int32 [128, 16, 2], P('seq', 'head'), may hold values from 0 to 7, all different within a row
- memory_blend_share: float32 [128, 16, 2], P('seq', 'head'), may hold values from 0.25 to 1
Outputs:
- mixed: bfloat16 [8192, 2048], P(('seq', 'head'))
Inputs may be any that keep to these rules, and one draw needn't show every extreme that they name: `routing`: each block and head names 2 different memories. `forget_rate`: positive rates.
All inputs are finite; a program needn't handle non-finite values.
Results may differ from a plain program's by a relative error of at most 0.03.
Values may be sent and summed in bfloat16 or wider, within the bound.
A program may use at most 128 MiB of HBM per device.

v0:
```python
import jax
import jax.numpy as jnp
from jax import lax
from jax.sharding import PartitionSpec as P

HD = 128
M = 8
CH = 64


HIGH = lax.Precision.HIGHEST


def carried_in(array, axis, combine, identity):
    size, index = (lax.axis_size(axis), lax.axis_index(axis))
    everything = jax.tree.map(lambda part: lax.all_gather(part, axis), array)
    start = jax.tree.map(
        lambda part, zero: jnp.broadcast_to(jnp.asarray(zero, part.dtype), part.shape),
        array,
        identity,
    )

    def hop(k, before):
        reached = k < index
        new = combine(before, jax.tree.map(lambda part: part[k], everything))
        return jax.tree.map(lambda a, b: jnp.where(reached, a, b), new, before)

    return lax.fori_loop(0, size, hop, start)


def per_device(
    tokens, w_query, w_key, w_value, w_out, norm_gain, forget_rate, routing, memory_blend_share
):
    tok_rows = tokens.shape[0]
    local_heads = w_query.shape[1] // HD
    num_blocks = tok_rows // CH

    def project(weight):
        return jnp.dot(tokens, weight, preferred_element_type=jnp.float32).astype(jnp.bfloat16)

    def split_heads(matrix):
        return matrix.reshape(num_blocks, CH, local_heads, HD).transpose(0, 2, 1, 3)

    query = split_heads(project(w_query))
    key_wide = split_heads(project(w_key)).astype(jnp.float32)
    key_rows = key_wide * lax.rsqrt(jnp.sum(key_wide * key_wide, axis=-1, keepdims=True) + 1e-06)
    key_short = key_rows.astype(jnp.bfloat16)
    value_rows = split_heads(project(w_value))
    retention_fades = forget_rate.reshape(num_blocks, CH, local_heads).transpose(0, 2, 1)
    cumul = jnp.cumsum(-retention_fades, axis=2)
    block_end = cumul[:, :, -1]
    positions = jnp.arange(CH)
    causal = positions[:, None] >= positions[None, :]
    gaps = cumul[:, :, :, None] - cumul[:, :, None, :]
    decays = jnp.where(causal, jnp.exp(jnp.where(causal, gaps, 0.0)), 0.0)
    scores = jnp.einsum("chqd,chkd->chqk", query, key_short, preferred_element_type=jnp.float32)
    weighted = (scores * decays).astype(jnp.bfloat16)
    within = jnp.einsum("chqk,chkd->chqd", weighted, value_rows, preferred_element_type=jnp.float32)
    scaled_keys = (
        key_short.astype(jnp.float32) * jnp.exp(block_end[:, :, None] - cumul)[..., None]
    ).astype(jnp.bfloat16)
    written = jnp.einsum(
        "chsd,chse->chde", scaled_keys, value_rows, preferred_element_type=jnp.float32
    )

    def advance(carried, inputs):
        product, memory = carried
        chosen, weights, ending, writing = inputs
        one_hot = (chosen[:, :, None] == jnp.arange(M)[None, None, :]).astype(jnp.float32)
        routed = jnp.sum(one_hot, axis=1)
        mix_weight = jnp.sum(weights[:, :, None] * one_hot, axis=1)
        mixed_state = jnp.einsum("hm,hmde->hde", mix_weight, memory, precision=HIGH)
        multiplier = mix_weight * product
        factor = jnp.where(routed > 0, jnp.exp(ending)[:, None], 1.0)
        memory = memory * factor[:, :, None, None] + routed[:, :, None, None] * writing[:, None]
        product = product * factor
        return ((product, memory), (mixed_state, multiplier))

    start_state = (
        jnp.ones((local_heads, M), jnp.float32),
        jnp.zeros((local_heads, M, HD, HD), jnp.float32),
    )
    (product, memory), (mixed_state, multiplier) = lax.scan(
        advance, start_state, (routing, memory_blend_share, block_end, written)
    )

    def combine(earlier, later):
        return (earlier[0] * later[0], later[0][:, :, None, None] * earlier[1] + later[1])

    incoming = carried_in(
        (product, memory), "seq", combine, (jnp.ones_like(product), jnp.zeros_like(memory))
    )[1]
    entering = jnp.einsum("chm,hmde->chde", multiplier, incoming, precision=HIGH)
    total_state = mixed_state + entering
    growth = jnp.exp(cumul)[..., None]
    attended_output = growth * jnp.einsum(
        "chqd,chde->chqe", query.astype(jnp.float32), total_state, precision=HIGH
    )
    attended_output = (
        attended_output + jnp.sum(memory_blend_share, axis=2)[:, :, None, None] * within
    )
    attended_output = attended_output.transpose(0, 2, 1, 3).reshape(tok_rows, local_heads, HD)
    normed = attended_output * lax.rsqrt(
        jnp.mean(attended_output * attended_output, axis=-1, keepdims=True) + 1e-06
    )
    normed = (
        (normed * norm_gain.reshape(local_heads, HD))
        .astype(jnp.bfloat16)
        .reshape(tok_rows, local_heads * HD)
    )
    exchanged = lax.all_to_all(normed, "head", split_axis=0, concat_axis=1, tiled=True)
    result = jnp.dot(
        exchanged,
        lax.all_gather(w_out, "head", axis=0, tiled=True),
        preferred_element_type=jnp.float32,
    )
    return result.astype(jnp.bfloat16)


def solution(mesh):
    placed = (
        P("seq", None),
        P(None, "head"),
        P(None, "head"),
        P(None, "head"),
        P("head", None),
        P("head"),
        P("seq", "head"),
        P("seq", "head", None),
        P("seq", "head", None),
    )
    return jax.shard_map(
        per_device, mesh=mesh, in_specs=placed, out_specs=P(("seq", "head"), None), check_vma=False
    )
```

profile of v0, /device:TPU:29, one launch (start us, length us, event | category | flops | bytes accessed | tf_op | source)
XLA Modules:
  0.0 581.3 jit_solution(14549176080145018837)
XLA Ops:
  9.3 5.5 convolution_convert_fusion.1
  16.7 5.8 %fusion.17 = f32[1024,512]{1,0:T(8,128)} fusion(bf16[1024,2048]{1,0:T(8,128)(2,1)} %param.13, bf16[2048,512]{1,0:T(8,128)(2,1)S(1)} %copy-done.10), kind=kOutput, calls=%fused_computation.39 | convolution fusion | flops 2148532224 | bytes 8388608 | tf_op jit(solution)/shard_map/dot_general | solution.py:39
  26.6 5.3 fusion.19
  32.0 236.1 %while.31 = (s32[]{:T(128)}, f32[4,8]{1,0:T(4,128)S(1)}, f32[4,8,128,128]{3,2,1,0:T(8,128)S(1)}, f32[16,4,128,128]{3,0,2,1:T(8,128)}, f32[16,4,8]{2,1,0:T(4,128)...) while((s32[]{:T(128)}, f32[4,8]{1,0:T(4,128)S(1)}, ...), condition=%wide.region_5.6_spmd.clone, body=%wide.region_2.5_spmd.clone.sunk | while | flops 8389059 | bytes 9969161 | solution.py:83
  35.6 2.8 fusion.63
  38.5 8.2 %dynamic_update_slice.14 = f32[16,4,128,128]{3,0,2,1:T(8,128)} dynamic-update-slice(f32[16,4,128,128]{3,0,2,1:T(8,128)} %get-tuple-element.406, f32[1,4,128,128]{3,0,2,1:T(1,128)S(1)} %fusion.63, s32[]{:T(128)S(6)} %copy.181, s32[]{:T(128)} %constant.63.clone.1..sunk, s32[]{:T(128)} %constant.63.clone.1..sunk, s32[]{:T(128)} %constant.63.clone.1..sunk) | dynamic-update-slice | bytes 524292 | tf_op jit(solution)/shard_map/while/body/jit(dynamic_update_index_in_dim)/dynamic_update_slice | solution.py:83
  50.4 2.8 fusion.63
  53.3 8.2 %dynamic_update_slice.14 = f32[16,4,128,128]{3,0,2,1:T(8,128)} dynamic-update-slice(f32[16,4,128,128]{3,0,2,1:T(8,128)} %get-tuple-element.406, f32[1,4,128,128]{3,0,2,1:T(1,128)S(1)} %fusion.63, s32[]{:T(128)S(6)} %copy.181, s32[]{:T(128)} %constant.63.clone.1..sunk, s32[]{:T(128)} %constant.63.clone.1..sunk, s32[]{:T(128)} %constant.63.clone.1..sunk) | dynamic-update-slice | bytes 524292 | tf_op jit(solution)/shard_map/while/body/jit(dynamic_update_index_in_dim)/dynamic_update_slice | solution.py:83
  65.2 2.8 fusion.63
  68.0 8.2 %dynamic_update_slice.14 = f32[16,4,128,128]{3,0,2,1:T(8,128)} dynamic-update-slice(f32[16,4,128,128]{3,0,2,1:T(8,128)} %get-tuple-element.406, f32[1,4,128,128]{3,0,2,1:T(1,128)S(1)} %fusion.63, s32[]{:T(128)S(6)} %copy.181, s32[]{:T(128)} %constant.63.clone.1..sunk, s32[]{:T(128)} %constant.63.clone.1..sunk, s32[]{:T(128)} %constant.63.clone.1..sunk) | dynamic-update-slice | bytes 524292 | tf_op jit(solution)/shard_map/while/body/jit(dynamic_update_index_in_dim)/dynamic_update_slice | solution.py:83
  79.9 2.8 fusion.63
  82.8 8.2 %dynamic_update_slice.14 = f32[16,4,128,128]{3,0,2,1:T(8,128)} dynamic-update-slice(f32[16,4,128,128]{3,0,2,1:T(8,128)} %get-tuple-element.406, f32[1,4,128,128]{3,0,2,1:T(1,128)S(1)} %fusion.63, s32[]{:T(128)S(6)} %copy.181, s32[]{:T(128)} %constant.63.clone.1..sunk, s32[]{:T(128)} %constant.63.clone.1..sunk, s32[]{:T(128)} %constant.63.clone.1..sunk) | dynamic-update-slice | bytes 524292 | tf_op jit(solution)/shard_map/while/body/jit(dynamic_update_index_in_dim)/dynamic_update_slice | solution.py:83
  94.7 2.8 fusion.63
  97.6 8.2 %dynamic_update_slice.14 = f32[16,4,128,128]{3,0,2,1:T(8,128)} dynamic-update-slice(f32[16,4,128,128]{3,0,2,1:T(8,128)} %get-tuple-element.406, f32[1,4,128,128]{3,0,2,1:T(1,128)S(1)} %fusion.63, s32[]{:T(128)S(6)} %copy.181, s32[]{:T(128)} %constant.63.clone.1..sunk, s32[]{:T(128)} %constant.63.clone.1..sunk, s32[]{:T(128)} %constant.63.clone.1..sunk) | dynamic-update-slice | bytes 524292 | tf_op jit(solution)/shard_map/while/body/jit(dynamic_update_index_in_dim)/dynamic_update_slice | solution.py:83
  109.5 2.8 fusion.63
  112.3 8.2 %dynamic_update_slice.14 = f32[16,4,128,128]{3,0,2,1:T(8,128)} dynamic-update-slice(f32[16,4,128,128]{3,0,2,1:T(8,128)} %get-tuple-element.406, f32[1,4,128,128]{3,0,2,1:T(1,128)S(1)} %fusion.63, s32[]{:T(128)S(6)} %copy.181, s32[]{:T(128)} %constant.63.clone.1..sunk, s32[]{:T(128)} %constant.63.clone.1..sunk, s32[]{:T(128)} %constant.63.clone.1..sunk) | dynamic-update-slice | bytes 524292 | tf_op jit(solution)/shard_map/while/body/jit(dynamic_update_index_in_dim)/dynamic_update_slice | solution.py:83
  124.2 2.8 fusion.63
  127.1 8.2 %dynamic_update_slice.14 = f32[16,4,128,128]{3,0,2,1:T(8,128)} dynamic-update-slice(f32[16,4,128,128]{3,0,2,1:T(8,128)} %get-tuple-element.406, f32[1,4,128,128]{3,0,2,1:T(1,128)S(1)} %fusion.63, s32[]{:T(128)S(6)} %copy.181, s32[]{:T(128)} %constant.63.clone.1..sunk, s32[]{:T(128)} %constant.63.clone.1..sunk, s32[]{:T(128)} %constant.63.clone.1..sunk) | dynamic-update-slice | bytes 524292 | tf_op jit(solution)/shard_map/while/body/jit(dynamic_update_index_in_dim)/dynamic_update_slice | solution.py:83
  139.0 2.8 fusion.63
  141.8 8.2 %dynamic_update_slice.14 = f32[16,4,128,128]{3,0,2,1:T(8,128)} dynamic-update-slice(f32[16,4,128,128]{3,0,2,1:T(8,128)} %get-tuple-element.406, f32[1,4,128,128]{3,0,2,1:T(1,128)S(1)} %fusion.63, s32[]{:T(128)S(6)} %copy.181, s32[]{:T(128)} %constant.63.clone.1..sunk, s32[]{:T(128)} %constant.63.clone.1..sunk, s32[]{:T(128)} %constant.63.clone.1..sunk) | dynamic-update-slice | bytes 524292 | tf_op jit(solution)/shard_map/while/body/jit(dynamic_update_index_in_dim)/dynamic_update_slice | solution.py:83
  153.7 2.8 fusion.63
  156.6 8.2 %dynamic_update_slice.14 = f32[16,4,128,128]{3,0,2,1:T(8,128)} dynamic-update-slice(f32[16,4,128,128]{3,0,2,1:T(8,128)} %get-tuple-element.406, f32[1,4,128,128]{3,0,2,1:T(1,128)S(1)} %fusion.63, s32[]{:T(128)S(6)} %copy.181, s32[]{:T(128)} %constant.63.clone.1..sunk, s32[]{:T(128)} %constant.63.clone.1..sunk, s32[]{:T(128)} %constant.63.clone.1..sunk) | dynamic-update-slice | bytes 524292 | tf_op jit(solution)/shard_map/while/body/jit(dynamic_update_index_in_dim)/dynamic_update_slice | solution.py:83
  168.5 2.8 fusion.63
  171.3 8.2 %dynamic_update_slice.14 = f32[16,4,128,128]{3,0,2,1:T(8,128)} dynamic-update-slice(f32[16,4,128,128]{3,0,2,1:T(8,128)} %get-tuple-element.406, f32[1,4,128,128]{3,0,2,1:T(1,128)S(1)} %fusion.63, s32[]{:T(128)S(6)} %copy.181, s32[]{:T(128)} %constant.63.clone.1..sunk, s32[]{:T(128)} %constant.63.clone.1..sunk, s32[]{:T(128)} %constant.63.clone.1..sunk) | dynamic-update-slice | bytes 524292 | tf_op jit(solution)/shard_map/while/body/jit(dynamic_update_index_in_dim)/dynamic_update_slice | solution.py:83
  183.2 2.8 fusion.63
  186.1 8.2 %dynamic_update_slice.14 = f32[16,4,128,128]{3,0,2,1:T(8,128)} dynamic-update-slice(f32[16,4,128,128]{3,0,2,1:T(8,128)} %get-tuple-element.406, f32[1,4,128,128]{3,0,2,1:T(1,128)S(1)} %fusion.63, s32[]{:T(128)S(6)} %copy.181, s32[]{:T(128)} %constant.63.clone.1..sunk, s32[]{:T(128)} %constant.63.clone.1..sunk, s32[]{:T(128)} %constant.63.clone.1..sunk) | dynamic-update-slice | bytes 524292 | tf_op jit(solution)/shard_map/while/body/jit(dynamic_update_index_in_dim)/dynamic_update_slice | solution.py:83
  197.9 2.8 fusion.63
  200.8 8.2 %dynamic_update_slice.14 = f32[16,4,128,128]{3,0,2,1:T(8,128)} dynamic-update-slice(f32[16,4,128,128]{3,0,2,1:T(8,128)} %get-tuple-element.406, f32[1,4,128,128]{3,0,2,1:T(1,128)S(1)} %fusion.63, s32[]{:T(128)S(6)} %copy.181, s32[]{:T(128)} %constant.63.clone.1..sunk, s32[]{:T(128)} %constant.63.clone.1..sunk, s32[]{:T(128)} %constant.63.clone.1..sunk) | dynamic-update-slice | bytes 524292 | tf_op jit(solution)/shard_map/while/body/jit(dynamic_update_index_in_dim)/dynamic_update_slice | solution.py:83
  212.7 2.8 fusion.63
  215.6 8.2 %dynamic_update_slice.14 = f32[16,4,128,128]{3,0,2,1:T(8,128)} dynamic-update-slice(f32[16,4,128,128]{3,0,2,1:T(8,128)} %get-tuple-element.406, f32[1,4,128,128]{3,0,2,1:T(1,128)S(1)} %fusion.63, s32[]{:T(128)S(6)} %copy.181, s32[]{:T(128)} %constant.63.clone.1..sunk, s32[]{:T(128)} %constant.63.clone.1..sunk, s32[]{:T(128)} %constant.63.clone.1..sunk) | dynamic-update-slice | bytes 524292 | tf_op jit(solution)/shard_map/while/body/jit(dynamic_update_index_in_dim)/dynamic_update_slice | solution.py:83
  227.5 2.8 fusion.63
  230.3 8.2 %dynamic_update_slice.14 = f32[16,4,128,128]{3,0,2,1:T(8,128)} dynamic-update-slice(f32[16,4,128,128]{3,0,2,1:T(8,128)} %get-tuple-element.406, f32[1,4,128,128]{3,0,2,1:T(1,128)S(1)} %fusion.63, s32[]{:T(128)S(6)} %copy.181, s32[]{:T(128)} %constant.63.clone.1..sunk, s32[]{:T(128)} %constant.63.clone.1..sunk, s32[]{:T(128)} %constant.63.clone.1..sunk) | dynamic-update-slice | bytes 524292 | tf_op jit(solution)/shard_map/while/body/jit(dynamic_update_index_in_dim)/dynamic_update_slice | solution.py:83
  242.2 2.8 fusion.63
  245.0 8.2 %dynamic_update_slice.14 = f32[16,4,128,128]{3,0,2,1:T(8,128)} dynamic-update-slice(f32[16,4,128,128]{3,0,2,1:T(8,128)} %get-tuple-element.406, f32[1,4,128,128]{3,0,2,1:T(1,128)S(1)} %fusion.63, s32[]{:T(128)S(6)} %copy.181, s32[]{:T(128)} %constant.63.clone.1..sunk, s32[]{:T(128)} %constant.63.clone.1..sunk, s32[]{:T(128)} %constant.63.clone.1..sunk) | dynamic-update-slice | bytes 524292 | tf_op jit(solution)/shard_map/while/body/jit(dynamic_update_index_in_dim)/dynamic_update_slice | solution.py:83
  256.9 2.8 fusion.63
  259.8 8.2 %dynamic_update_slice.14 = f32[16,4,128,128]{3,0,2,1:T(8,128)} dynamic-update-slice(f32[16,4,128,128]{3,0,2,1:T(8,128)} %get-tuple-element.406, f32[1,4,128,128]{3,0,2,1:T(1,128)S(1)} %fusion.63, s32[]{:T(128)S(6)} %copy.181, s32[]{:T(128)} %constant.63.clone.1..sunk, s32[]{:T(128)} %constant.63.clone.1..sunk, s32[]{:T(128)} %constant.63.clone.1..sunk) | dynamic-update-slice | bytes 524292 | tf_op jit(solution)/shard_map/while/body/jit(dynamic_update_index_in_dim)/dynamic_update_slice | solution.py:83
  270.2 6.2 %convolution_convert_fusion.3 = bf16[1024,512]{1,0:T(8,128)(2,1)} fusion(bf16[1024,2048]{1,0:T(8,128)(2,1)} %param.13, bf16[2048,512]{1,0:T(8,128)(2,1)} %param.14), kind=kOutput, calls=%fused_computation.40 | convolution fusion | flops 2148007936 | bytes 7340032 | tf_op jit(solution)/shard_map/dot_general | solution.py:39
  278.6 23.4 %all-gather.2 = f32[8,4,8]{2,1,0:T(4,128)S(1)} all-gather(f32[1,4,8]{2,1,0:T(4,128)S(1)} %bitcast.103), channel_id=2, replica_groups=mesh['seq'=8,'head'=4] {'seq'}, dimensions={0}, use_global_device_ids=true | all-gather | bytes 1152 | tf_op jit(solution)/shard_map/all_gather | solution.py:16
  302.0 4.4 fusion.18
  306.4 188.7 %all-gather.8.cloned.1.call-done = f32[32,8,128,128]{3,2,1,0:T(8,128)} async-done(((f32[4,8,128,128]{3,2,1,0:T(8,128)}), f32[32,8,128,128]{3,2,1,0:T(8,128)}) %all-gather.8.cloned.1.call-update) | async-done | bytes 16777232 | tf_op jit(solution)/shard_map/all_gather | solution.py:16
  495.1 18.3 %while.32 = (s32[]{:T(128)}, f32[4,8,128,128]{3,2,1,0:T(8,128)S(1)}, s32[]{:T(128)}, f32[8,4,8]{2,1,0:T(4,128)S(1)}, f32[8,4,8,128,128]{4,3,2,1,0:T(8,128)}, /*index=5*/s32[]{:T(128)}, s32[]{:T(128)}) while((s32[]{:T(128)}, f32[4,8,128,128]{3,2,1,0:T(8,128)S(1)}, s32[]{:T(128)}, f32[8,4,8]{2,1,0:T(4,128)S(1)}, ...), condition=%wide.region_7.8_spmd.clone, body=%wide.region_6.7_spmd.clone.sunk | while | flops 2097156 | bytes 6291953 | solution.py:28
  508.5 2.7 fusion.64
  513.4 6.1 %bitcast_add_fusion.1 = f32[16,4,128,128]{3,0,2,1:T(8,128)S(1)} fusion(f32[16,4,128,128]{3,0,2,1:T(8,128)} %get-tuple-element.149, f32[4,8,128,128]{3,2,1,0:T(8,128)S(1)} %get-tuple-element.152, f32[16,4,8,1]{2,1,0,3:T(4,128)S(1)} %bitcast.105), kind=kOutput, calls=%fused_computation.22 | convolution fusion | flops 101711872 | bytes 10487808 | tf_op jit(solution)/shard_map/chm,hmde->chde/dot_general | solution.py:93
  519.5 4.0 multiply_reduce_fusion
  523.5 2.7 copy.110
  530.9 3.1 mul.145
  536.2 28.3 %all_to_all.16 = bf16[4,256,512]{2,1,0:T(8,128)(2,1)S(1)} all-to-all(bf16[4,256,512]{2,1,0:T(8,128)(2,1)S(1)} %multiply_convert_fusion), channel_id=1, replica_groups=mesh['seq'=8,'head'=4] {'head'}, dimensions={0} | all-to-all | bytes 2097152 | tf_op jit(solution)/shard_map/all_to_all | solution.py:111
  567.6 6.8 %convolution_convert_fusion = bf16[256,2048]{1,0:T(8,128)(2,1)} fusion(bf16[256,2048]{0,1:T(8,128)(2,1)S(1)} %bitcast.98, bf16[2048,2048]{1,0:T(8,128)(2,1)} %all-gather.6.cloned.1.call-done), kind=kOutput, calls=%fused_computation.25 | convolution fusion | flops 2148007936 | bytes 10485760 | tf_op jit(solution)/shard_map/dot_general | solution.py:112
  (200 shorter events, 96.5 us)
Async XLA Ops:
  6.5 2.8 copy-start
  6.5 488.6 %all-gather.8.cloned.1.call-start = ((), (), s32[]{:S(2)}) async-start(), calls=%async_computation.2 | async-start | bytes 18874368 | tf_op jit(solution)/shard_map/all_gather | solution.py:16
  14.8 1.9 copy-start.10
  24.5 1.4 copy-start.4
  24.5 0.7 copy-start.8
  24.5 1.4 copy-start.7
  26.6 5.3 copy-start.2
  268.0 1.3 copy-start.3
  269.4 298.2 %all-gather.6.cloned.1.call-start = ((), (), s32[]{:S(2)}) async-start(), calls=%async_computation.1 | async-start | bytes 10485760 | tf_op jit(solution)/shard_map/all_gather | solution.py:114
  513.4 6.1 %copy-start.5 = (bf16[16,64,4,128]{3,2,1,0:T(4,128)(2,1)S(1)}, bf16[16,64,4,128]{3,2,1,0:T(4,128)(2,1)}, u32[]{:S(2)}) copy-start(bf16[16,64,4,128]{3,2,1,0:T(4,128)(2,1)} %reshape.95) | copy-start | bytes 3145732
  513.4 6.1 %copy-start.6 = (f32[16,4,64,128]{3,2,1,0:T(8,128)S(1)}, f32[16,4,64,128]{3,2,1,0:T(8,128)}, u32[]{:S(2)}) copy-start(f32[16,4,64,128]{3,2,1,0:T(8,128)} %fusion.18) | copy-start | bytes 6291460
  530.9 3.1 copy-start.9
  567.6 6.9 %copy-start.1 = (bf16[2048,512]{1,0:T(8,128)(2,1)S(1)}, bf16[2048,512]{1,0:T(8,128)(2,1)}, u32[]{:S(2)}) copy-start(bf16[2048,512]{1,0:T(8,128)(2,1)} %param.16) | copy-start | bytes 6291460
Sparse Core Ops, SparseCore 0:
  269.5 225.5 all-gather.7
  496.7 70.8 all-gather.5
where the time goes:
time: 586 us; the launch traced here: 581 us
  local copies, waits for them, and re-layouts  201 us (34%)
  waiting for transfers between devices  192 us (33%)
  matrix products  89.6 us (15%)
  blocking collectives  51.8 us (9%)
  other arithmetic  33 us (6%)
  between operations  13.6 us (2%)
    all_gather x1, waiting for transfers between devices, carried_in(): everything = jax.tree.map(lambda part: lax.all_gather(part, axis), array)  189 us
    dynamic_update_slice x16, local copies, waits for them, and re-layouts, per_device(): lax.scan(advance, start_state, (routing, memory_blend_share, block_end, w...  132 us
    dot_general x16, matrix products, advance(): mixed_state = jnp.einsum('hm,hmde->hde', mix_weight, memory, precision=HIGH)  45.6 us
    all_to_all x1, blocking collectives, per_device(): lax.all_to_all(normed, 'head', split_axis=0, concat_axis=1, tiled=True)  28.3 us
    all_gather x1, blocking collectives, carried_in(): everything = jax.tree.map(lambda part: lax.all_gather(part, axis), array)  23.4 us
    select_n x8, other arithmetic, hop(): return jax.tree.map(lambda a, b: jnp.where(reached, a, b), new, before)  18 us
    dot_general x3, matrix products, project(): jnp.dot(tokens, weight, preferred_element_type=jnp.float32)  17.5 us
    mul x16, local copies, waits for them, and re-layouts, advance(): routed[:, :, None, None] * writing[:, None]  15.6 us
  transfers between devices with their start and end apart: 2, of which 2 were waited for; matrix products, arithmetic and copies ran while one was open for 9% of the time, Pallas kernels for 0%

commit v1 on v0

v1 whole, which is shorter than its diff:
```python
import functools

import jax
import jax.numpy as jnp
from jax import lax
from jax.experimental import pallas as pl
from jax.experimental.pallas import tpu as pltpu
from jax.sharding import PartitionSpec as P

HD = 128
M = 8
CH = 64

HIGH = lax.Precision.HIGHEST
MESH = pl.DeviceIdType.MESH
VMEM = pltpu.VMEM
SMEM = pltpu.SMEM
LIMIT = 60 * 1024 * 1024


def local_kernel(
    chosen, shares, fades, q_ref, k_ref, v_ref, column_ref, row_ref, att_ref, mem_ref
):
    blocks, local_heads = row_ref.shape[0], row_ref.shape[1]
    mem_ref[...] = jnp.zeros_like(mem_ref)
    t = lax.broadcasted_iota(jnp.int32, (CH, CH), 0)
    s = lax.broadcasted_iota(jnp.int32, (CH, CH), 1)
    causal = t >= s

    def block(b, carry):
        rows = pl.ds(pl.multiple_of(b * CH, CH), CH)
        for h in range(local_heads):
            cols = slice(h * HD, (h + 1) * HD)
            query = q_ref[rows, cols]
            wide = k_ref[rows, cols].astype(jnp.float32)
            values = v_ref[rows, cols]
            keys = wide * lax.rsqrt(jnp.sum(wide * wide, axis=-1, keepdims=True) + 1e-06)
            keys = keys.astype(jnp.bfloat16)
            column = column_ref[rows, h : h + 1]
            line = row_ref[b, h : h + 1, :]
            gaps = jnp.where(causal, column - line, 0.0)
            decays = jnp.where(causal, jnp.exp(gaps), 0.0)
            scores = lax.dot_general(
                query, keys, (((1,), (1,)), ((), ())), preferred_element_type=jnp.float32
            )
            weighted = (scores * decays).astype(jnp.bfloat16)
            within = jnp.dot(weighted, values, preferred_element_type=jnp.float32)
            ending = column[CH - 1 : CH]
            scaled = (keys.astype(jnp.float32) * jnp.exp(ending - column)).astype(jnp.bfloat16)
            written = lax.dot_general(
                scaled, values, (((0,), (0,)), ((), ())), preferred_element_type=jnp.float32
            )
            at = (b * local_heads + h) * 2
            first, second = chosen[at], chosen[at + 1]
            share_a, share_b = shares[at], shares[at + 1]
            fade = fades[b * local_heads + h]
            old_a = mem_ref[h * M + first]
            old_b = mem_ref[h * M + second]
            mixed = (share_a * old_a + share_b * old_b).astype(jnp.bfloat16)
            carried = jnp.dot(query, mixed, preferred_element_type=jnp.float32)
            att_ref[rows, cols] = jnp.exp(column) * carried + (share_a + share_b) * within
            mem_ref[h * M + first] = fade * old_a + written
            mem_ref[h * M + second] = fade * old_b + written
        return carry

    lax.fori_loop(0, blocks, block, 0)


def chain_kernel(
    chosen,
    multipliers,
    products,
    mem_ref,
    q_ref,
    column_ref,
    att_ref,
    gain_ref,
    out_ref,
    inbox,
    outbox,
    current,
    send_sem,
    recv_sem,
):
    size, me = lax.axis_size("seq"), lax.axis_index("seq")
    pieces = mem_ref.shape[0]
    local_heads = pieces // M
    blocks = q_ref.shape[0] // CH
    barrier = pltpu.get_barrier_semaphore()

    @pl.when(me > 0)
    def _():
        pl.semaphore_signal(barrier, 1, device_id={"seq": me - 1}, device_id_type=MESH)

    @pl.when(me < size - 1)
    def _():
        pl.semaphore_signal(barrier, 1, device_id={"seq": me + 1}, device_id_type=MESH)

    peers = jnp.where(me > 0, 1, 0) + jnp.where(me < size - 1, 1, 0)
    pl.semaphore_wait(barrier, peers)

    @pl.when(me == 0)
    def _():
        inbox[...] = jnp.zeros_like(inbox)

    def copy(c):
        return pltpu.make_async_remote_copy(
            src_ref=outbox.at[c],
            dst_ref=inbox.at[c],
            send_sem=send_sem.at[c],
            recv_sem=recv_sem.at[c],
            device_id={"seq": me + 1},
            device_id_type=MESH,
        )

    for h in range(local_heads):

        def pass_on(m, carry):
            c = h * M + m

            @pl.when(me > 0)
            def _():
                copy(c).wait_recv()

            arrived = inbox[c].astype(jnp.float32)
            current[m] = arrived

            @pl.when(me < size - 1)
            def _():
                outbox[c] = (products[c] * arrived + mem_ref[c]).astype(jnp.bfloat16)
                copy(c).start()

            return carry

        lax.fori_loop(0, M, pass_on, 0)
        cols = slice(h * HD, (h + 1) * HD)

        def block(b, carry):
            rows = pl.ds(pl.multiple_of(b * CH, CH), CH)
            at = (b * local_heads + h) * 2
            entering = (
                multipliers[at] * current[chosen[at]]
                + multipliers[at + 1] * current[chosen[at + 1]]
            ).astype(jnp.bfloat16)
            carried = jnp.dot(q_ref[rows, cols], entering, preferred_element_type=jnp.float32)
            total = att_ref[rows, cols] + jnp.exp(column_ref[rows, h : h + 1]) * carried
            scale = lax.rsqrt(jnp.mean(total * total, axis=-1, keepdims=True) + 1e-06)
            out_ref[rows, cols] = (total * scale * gain_ref[:, cols]).astype(jnp.bfloat16)
            return carry

        lax.fori_loop(0, blocks, block, 0, unroll=4)

    @pl.when(me < size - 1)
    def _():
        def drain(c, carry):
            copy(c).wait_send()
            return carry

        lax.fori_loop(0, pieces, drain, 0)


def per_device(
    tokens, w_query, w_key, w_value, w_out, norm_gain, forget_rate, routing, memory_blend_share
):
    tok_rows = tokens.shape[0]
    local_heads = w_query.shape[1] // HD
    num_blocks = tok_rows // CH
    width = local_heads * HD
    whole_out = lax.all_gather(w_out, "head", axis=0, tiled=True)

    def project(weight):
        return jnp.dot(tokens, weight, preferred_element_type=jnp.float32).astype(jnp.bfloat16)

    key_raw, value_rows, query = project(w_key), project(w_value), project(w_query)
    cumul = jnp.cumsum(-forget_rate.reshape(num_blocks, CH, local_heads), axis=1)
    block_end = cumul[:, -1]
    column = cumul.reshape(tok_rows, local_heads)
    row = cumul.transpose(0, 2, 1)
    one_hot = (routing[..., None] == jnp.arange(M)).astype(jnp.float32)
    ends = jnp.sum(one_hot, axis=2) * block_end[:, :, None]
    before = jnp.arange(num_blocks)[:, None] > jnp.arange(num_blocks)[None, :]
    earlier = jnp.sum(jnp.where(before[:, :, None, None], ends[None], 0.0), axis=1)
    multipliers = memory_blend_share * jnp.sum(one_hot * jnp.exp(earlier)[:, :, None], axis=-1)
    products = jnp.exp(jnp.sum(ends, axis=0)).reshape(-1)
    chosen = routing.reshape(-1)

    smem = pl.BlockSpec(memory_space=SMEM)
    vmem = pl.BlockSpec(memory_space=VMEM)
    attended, memory = pl.pallas_call(
        local_kernel,
        out_shape=(
            jax.ShapeDtypeStruct((tok_rows, width), jnp.float32),
            jax.ShapeDtypeStruct((local_heads * M, HD, HD), jnp.float32),
        ),
        in_specs=[smem] * 3 + [vmem] * 5,
        out_specs=(vmem, vmem),
        compiler_params=pltpu.CompilerParams(vmem_limit_bytes=LIMIT),
        name="local",
    )(
        chosen,
        memory_blend_share.reshape(-1),
        jnp.exp(block_end).reshape(-1),
        query,
        key_raw,
        value_rows,
        column,
        row,
    )
    pieces = local_heads * M
    normed = pl.pallas_call(
        chain_kernel,
        out_shape=jax.ShapeDtypeStruct((tok_rows, width), jnp.bfloat16),
        in_specs=[smem] * 3 + [vmem] * 5,
        out_specs=vmem,
        scratch_shapes=[
            VMEM((pieces, HD, HD), jnp.bfloat16),
            VMEM((pieces, HD, HD), jnp.bfloat16),
            VMEM((M, HD, HD), jnp.float32),
            pltpu.SemaphoreType.DMA((pieces,)),
            pltpu.SemaphoreType.DMA((pieces,)),
        ],
        compiler_params=pltpu.CompilerParams(
            collective_id=0, has_side_effects=True, vmem_limit_bytes=LIMIT
        ),
        name="chain",
    )(chosen, multipliers.reshape(-1), products, memory, query, column, attended, norm_gain[None])
    exchanged = lax.all_to_all(normed, "head", split_axis=0, concat_axis=1, tiled=True)
    result = jnp.dot(exchanged, whole_out, preferred_element_type=jnp.float32)
    return result.astype(jnp.bfloat16)


def solution(mesh):
    placed = (
        P("seq", None),
        P(None, "head"),
        P(None, "head"),
        P(None, "head"),
        P("head", None),
        P("head"),
        P("seq", "head"),
        P("seq", "head", None),
        P("seq", "head", None),
    )
    return jax.shard_map(
        per_device, mesh=mesh, in_specs=placed, out_specs=P(("seq", "head"), None), check_vma=False
    )
```

time: 586 us -> 130 us (0.22)
  local copies, waits for them, and re-layouts: 201 us -> 8.48 us
  waiting for transfers between devices: 192 us -> 0.71 us
  matrix products: 89.6 us -> 20.1 us
  Pallas kernels: 0 us -> 59.3 us
  blocking collectives: 51.8 us -> 21.2 us
  other arithmetic: 33 us -> 6.64 us
    all_gather x2 -> x1, waiting for transfers between devices: 191 us -> 0.01 us  [per_device(): whole_out = lax.all_gather(w_out, 'head', axis=0, tiled=True)]
    dynamic_update_slice x16 -> x0, local copies, waits for them, and re-layouts: 132 us -> none  [per_device(): lax.scan(advance, start_state, (routing, memory_blend_share, block_end, w...]
    dot_general x21 -> x1, matrix products: 72.1 us -> 6.7 us  [per_device(): result = jnp.dot(exchanged, whole_out, preferred_element_type=jnp.float32)]
    pallas_call x0 -> x2, Pallas kernels: none -> 59.3 us  [the longest x1 45.2 us: per_device(): pl.pallas_call(chain_kernel, out_shape=jax.ShapeDtypeStruct((tok_rows, wi...]
    mul x42 -> x1, local copies, waits for them, and re-layouts: 31.5 us -> 0.11 us  [per_device(): memory_blend_share * jnp.sum(one_hot * jnp.exp(earlier)[:, :, None], axis...]
    all_gather x1 -> x0, blocking collectives: 23.4 us -> none  [carried_in(): everything = jax.tree.map(lambda part: lax.all_gather(part, axis), array)]
    select_n x8 -> x0, other arithmetic: 18 us -> none  [hop(): return jax.tree.map(lambda a, b: jnp.where(reached, a, b), new, before)]
    eq x16 -> x0, local copies, waits for them, and re-layouts: 10.9 us -> none  [advance(): chosen[:, :, None] == jnp.arange(M)[None, None, :]]
  transfers between devices with their start and end apart: 2 -> 1, of which waited for: 2 -> 0; matrix products, arithmetic and copies ran while one was open for 9% -> 22% of each run, Pallas kernels for 0% -> 46%
where the time goes in v1:
time: 130 us
  Pallas kernels  59.3 us (46%)
  blocking collectives  21.2 us (16%)
  matrix products  20.1 us (15%)
  between operations  13.5 us (10%)
  local copies, waits for them, and re-layouts  8.48 us (7%)
  other arithmetic  6.64 us (5%)
    pallas_call x1, Pallas kernels, per_device(): pl.pallas_call(chain_kernel, out_shape=jax.ShapeDtypeStruct((tok_rows, wi...  45.2 us
    all_to_all x1, blocking collectives, per_device(): lax.all_to_all(normed, 'head', split_axis=0, concat_axis=1, tiled=True)  21.2 us
    pallas_call x1, Pallas kernels, per_device(): pl.pallas_call(local_kernel, out_shape=(jax.ShapeDtypeStruct((tok_rows, w...  14.1 us
    dot_general x3, matrix products, project(): jnp.dot(tokens, weight, preferred_element_type=jnp.float32)  13.4 us
    dot_general x1, matrix products, per_device(): result = jnp.dot(exchanged, whole_out, preferred_element_type=jnp.float32)  6.7 us
    another operation x1, other arithmetic, per_device(): jnp.cumsum(-forget_rate.reshape(num_blocks, CH, local_heads), axis=1)  6.33 us
  transfers between devices with their start and end apart: 1, of which 0 were waited for; matrix products, arithmetic and copies ran while one was open for 22% of the time, Pallas kernels for 46%

profile of v1, /device:TPU:29, one launch (start us, length us, event | category | flops | bytes accessed | tf_op | source)
XLA Modules:
  0.0 129.8 jit_solution(4254825457736737428)
XLA Ops:
  6.5 0.0 copy-start
  6.5 0.0 copy-start.3
  6.5 0.0 all-gather.2.cloned.1.call-start
  6.5 0.7 all-gather.2.cloned.1.call-update
  7.3 0.1 copy-done.3
  7.4 0.0 copy-start.1
  7.4 0.0 copy-start.2
  7.4 0.1 neg.7
  7.5 0.3 copy.39
  7.8 6.3 %fusion.1 = f32[16,64,4]{2,0,1:T(8,128)S(1)} fusion(f32[16,64,4]{2,0,1:T(8,128)S(1)} %copy.39), kind=kOutput, calls=%fused_computation.12 | output fusion | flops 258048 | bytes 32768 | tf_op jit(solution)/shard_map/jit(cumsum)/reduce_window_sum | solution.py:175
  14.2 1.0 copy.44
  15.1 0.9 copy.45
  16.0 0.7 exp.25.fades
  16.7 0.0 copy-done.1
  16.7 0.1 copy.38
  16.8 0.7 reshape.43.chosen
  17.5 0.0 copy-done.2
  17.5 0.1 copy.43
  17.6 0.7 reshape.45.shares
  18.3 0.1 copy.40
  18.4 0.1 fusion
  18.4 0.2 select_reduce_fusion
  18.6 0.1 copy.41
  18.8 0.1 copy.42
  18.9 0.6 reshape.44.multipliers
  19.5 0.7 exp.23.products
  20.2 0.0 copy-done
  20.2 0.0 copy-start.4
  20.2 0.0 copy-start.5
  20.2 6.7 %convolution_convert_fusion.3.q_ref = bf16[1024,512]{1,0:T(8,128)(2,1)} fusion(bf16[1024,2048]{1,0:T(8,128)(2,1)} %param.9, bf16[2048,512]{1,0:T(8,128)(2,1)S(1)} %copy-done), kind=kOutput, calls=%fused_computation.3 | convolution fusion | flops 2148007936 | bytes 7340032 | tf_op jit(solution)/shard_map/dot_general | solution.py:172
  26.9 0.0 copy-done.4
  26.9 0.0 copy-done.5
  26.9 0.0 copy-start.6
  26.9 3.3 %convolution_convert_fusion.1.v_ref = bf16[1024,512]{1,0:T(8,128)(2,1)} fusion(bf16[1024,2048]{1,0:T(8,128)(2,1)S(1)} %copy-done.4, bf16[2048,512]{1,0:T(8,128)(2,1)S(1)} %copy-done.5), kind=kOutput, calls=%fused_computation.1 | convolution fusion | flops 2148007936 | bytes 7340032 | tf_op jit(solution)/shard_map/dot_general | solution.py:172
  30.2 0.0 copy-done.6
  30.2 3.4 %convolution_convert_fusion.2.k_ref = bf16[1024,512]{1,0:T(8,128)(2,1)} fusion(bf16[1024,2048]{1,0:T(8,128)(2,1)S(1)} %copy-done.4, bf16[2048,512]{1,0:T(8,128)(2,1)S(1)} %copy-done.6), kind=kOutput, calls=%fused_computation.2 | convolution fusion | flops 2148007936 | bytes 7340032 | tf_op jit(solution)/shard_map/dot_general | solution.py:172
  33.6 14.1 %local.1 = (f32[1024,512]{1,0:T(8,128)}, f32[32,128,128]{2,1,0:T(8,128)}) custom-call(s32[128]{0:T(128)} %reshape.43.chosen, f32[128]{0:T(128)} %reshape.45.shares, f32[64]{0:T(128)} %exp.25.fades, bf16[1024,512]{1,0:T(8,128)(2,1)} %convolution_convert_fusion.3.q_ref, bf16[1024,512]{1,0:T(8,128)(2,1)} %convolution_convert_fusion.2.k_ref, ...), custom_call_target="tpu_custom_call" | custom-call | tf_op jit(solution)/shard_map/local/pallas_call | solution.py:189
  47.7 45.2 %chain.1 = bf16[1024,512]{1,0:T(8,128)(2,1)} custom-call(s32[128]{0:T(128)} %reshape.43.chosen, f32[128]{0:T(128)} %reshape.44.multipliers, f32[32]{0:T(128)} %exp.23.products, f32[32,128,128]{2,1,0:T(8,128)} %get-tuple-element.7.mem_ref, bf16[1024,512]{1,0:T(8,128)(2,1)} %convolution_convert_fusion.3.q_ref, f32[1024,4]{1,0:T(8,128)} %bitcast.23, ...), custom_call_target="tpu_custom_call" | custom-call | tf_op jit(solution)/shard_map/chain/pallas_call | solution.py:210
  92.9 2.3 %copy.46 = bf16[4,256,512]{1,2,0:T(8,128)(2,1)} copy(bf16[4,256,512]{2,1,0:T(8,128)(2,1)} %bitcast.24) | data formatting | bytes 2097152 | tf_op jit(solution)/shard_map/all_to_all | solution.py:227
  95.1 21.2 %all_to_all.19 = bf16[4,256,512]{1,2,0:T(8,128)(2,1)S(1)} all-to-all(bf16[4,256,512]{1,2,0:T(8,128)(2,1)} %copy.46), channel_id=1, replica_groups=mesh['seq'=8,'head'=4] {'head'}, dimensions={0} | all-to-all | bytes 2097152 | tf_op jit(solution)/shard_map/all_to_all | solution.py:227
  116.3 0.0 all-gather.2.cloned.1.call-done
  116.3 6.7 %convolution_convert_fusion = bf16[256,2048]{1,0:T(8,128)(2,1)} fusion(bf16[256,2048]{0,1:T(8,128)(2,1)S(1)} %bitcast.21, bf16[2048,2048]{1,0:T(8,128)(2,1)} %all-gather.2.cloned.1.call-done), kind=kOutput, calls=%fused_computation | convolution fusion | flops 2148007936 | bytes 10485760 | tf_op jit(solution)/shard_map/dot_general | solution.py:228
  (8 shorter events, 0.1 us)
Async XLA Ops:
  6.5 13.6 %copy-start = (bf16[2048,512]{1,0:T(8,128)(2,1)S(1)}, bf16[2048,512]{1,0:T(8,128)(2,1)}, u32[]{:S(2)}) copy-start(bf16[2048,512]{1,0:T(8,128)(2,1)} %param.10) | copy-start | bytes 6291460
  6.5 0.9 copy-start.3
  6.5 109.7 %all-gather.2.cloned.1.call-start = ((), (), s32[]{:S(2)}) async-start(), calls=%async_computation.1 | async-start | bytes 10485760 | tf_op jit(solution)/shard_map/all_gather | solution.py:169
  7.4 9.3 %copy-start.1 = (s32[16,4,2]{0,2,1:T(2,128)S(1)}, s32[16,4,2]{0,2,1:T(2,128)}, u32[]{:S(2)}) copy-start(s32[16,4,2]{0,2,1:T(2,128)} %param.16) | copy-start | bytes 1540
  7.4 10.1 %copy-start.2 = (f32[16,4,2]{0,2,1:T(2,128)S(1)}, f32[16,4,2]{0,2,1:T(2,128)}, u32[]{:S(2)}) copy-start(f32[16,4,2]{0,2,1:T(2,128)} %param.17) | copy-start | bytes 1540
  20.2 6.7 %copy-start.4 = (bf16[1024,2048]{1,0:T(8,128)(2,1)S(1)}, bf16[1024,2048]{1,0:T(8,128)(2,1)}, u32[]{:S(2)}) copy-start(bf16[1024,2048]{1,0:T(8,128)(2,1)} %param.9) | copy-start | bytes 12582916
  20.2 6.7 %copy-start.5 = (bf16[2048,512]{1,0:T(8,128)(2,1)S(1)}, bf16[2048,512]{1,0:T(8,128)(2,1)}, u32[]{:S(2)}) copy-start(bf16[2048,512]{1,0:T(8,128)(2,1)} %param.12) | copy-start | bytes 6291460
  26.9 3.3 %copy-start.6 = (bf16[2048,512]{1,0:T(8,128)(2,1)S(1)}, bf16[2048,512]{1,0:T(8,128)(2,1)}, u32[]{:S(2)}) copy-start(bf16[2048,512]{1,0:T(8,128)(2,1)} %param.11) | copy-start | bytes 6291460
Sparse Core Ops, SparseCore 0:
  8.9 59.5 all-gather.1

commit v2 on v1

v2 whole, which is shorter than its diff:
```python
import jax
import jax.numpy as jnp
from jax import lax
from jax.experimental import pallas as pl
from jax.experimental.pallas import tpu as pltpu
from jax.sharding import PartitionSpec as P

HD = 128
M = 8
CH = 64

HIGH = lax.Precision.HIGHEST
MESH = pl.DeviceIdType.MESH
VMEM = pltpu.VMEM
SMEM = pltpu.SMEM
LIMIT = 60 * 1024 * 1024


def local_kernel(
    chosen, shares, q_ref, k_ref, v_ref, rate_ref, att_ref, mem_ref, growth_ref, entry_ref, prod_ref
):
    tok_rows, local_heads = rate_ref.shape
    blocks = tok_rows // CH
    mem_ref[...] = jnp.zeros_like(mem_ref)
    prod_ref[...] = jnp.ones_like(prod_ref)
    t = lax.broadcasted_iota(jnp.int32, (CH, CH), 0)
    s = lax.broadcasted_iota(jnp.int32, (CH, CH), 1)
    causal = t >= s

    def block(b, carry):
        rows = pl.ds(pl.multiple_of(b * CH, CH), CH)
        rates = rate_ref[rows, :]
        columns = -jnp.dot(
            jnp.where(t >= s, 1.0, 0.0), rates, precision=HIGH, preferred_element_type=jnp.float32
        )
        lines = -lax.dot_general(
            rates,
            jnp.where(t <= s, 1.0, 0.0),
            (((0,), (0,)), ((), ())),
            precision=HIGH,
            preferred_element_type=jnp.float32,
        )
        growths = jnp.exp(columns)
        growth_ref[rows, :] = growths
        for h in range(local_heads):
            cols = slice(h * HD, (h + 1) * HD)
            query = q_ref[rows, cols]
            wide = k_ref[rows, cols].astype(jnp.float32)
            values = v_ref[rows, cols]
            keys = wide * lax.rsqrt(jnp.sum(wide * wide, axis=-1, keepdims=True) + 1e-06)
            keys = keys.astype(jnp.bfloat16)
            column = columns[:, h : h + 1]
            line = lines[h : h + 1, :]
            gaps = jnp.where(causal, column - line, 0.0)
            decays = jnp.where(causal, jnp.exp(gaps), 0.0)
            scores = lax.dot_general(
                query, keys, (((1,), (1,)), ((), ())), preferred_element_type=jnp.float32
            )
            weighted = (scores * decays).astype(jnp.bfloat16)
            within = jnp.dot(weighted, values, preferred_element_type=jnp.float32)
            ending = column[CH - 1 : CH]
            scaled = (keys.astype(jnp.float32) * jnp.exp(ending - column)).astype(jnp.bfloat16)
            written = lax.dot_general(
                scaled, values, (((0,), (0,)), ((), ())), preferred_element_type=jnp.float32
            )
            at = (b * local_heads + h) * 2
            first, second = h * M + chosen[at], h * M + chosen[at + 1]
            share_a, share_b = shares[at], shares[at + 1]
            fade = jnp.broadcast_to(growths[CH - 1 : CH, h : h + 1], (1, HD))
            old_a = mem_ref[first]
            old_b = mem_ref[second]
            mixed = (share_a * old_a + share_b * old_b).astype(jnp.bfloat16)
            carried = jnp.dot(query, mixed, preferred_element_type=jnp.float32)
            att_ref[rows, cols] = (
                growths[:, h : h + 1] * carried + (share_a + share_b) * within
            )
            mem_ref[first] = fade * old_a + written
            mem_ref[second] = fade * old_b + written
            prod_a, prod_b = prod_ref[first], prod_ref[second]
            entry_ref[at] = share_a * prod_a
            entry_ref[at + 1] = share_b * prod_b
            prod_ref[first] = fade * prod_a
            prod_ref[second] = fade * prod_b
        return carry

    lax.fori_loop(0, blocks, block, 0)


def chain_kernel(
    chosen,
    entry_ref,
    prod_ref,
    mem_ref,
    q_ref,
    growth_ref,
    att_ref,
    gain_ref,
    w_hbm,
    out_ref,
    inbox,
    outbox,
    current,
    finished,
    exchanged,
    partial,
    w_ref,
    w_sem,
    send_sem,
    recv_sem,
    row_send,
    row_recv,
):
    size, me = lax.axis_size("seq"), lax.axis_index("seq")
    groups, mine = lax.axis_size("head"), lax.axis_index("head")
    pieces = mem_ref.shape[0]
    local_heads = pieces // M
    width = local_heads * HD
    blocks = q_ref.shape[0] // CH
    own_rows = q_ref.shape[0] // groups
    fetch = pltpu.make_async_copy(w_hbm, w_ref, w_sem)
    fetch.start()
    barrier = pltpu.get_barrier_semaphore()

    @pl.when(me > 0)
    def _():
        pl.semaphore_signal(barrier, 1, device_id={"seq": me - 1}, device_id_type=MESH)

    @pl.when(me < size - 1)
    def _():
        pl.semaphore_signal(barrier, 1, device_id={"seq": me + 1}, device_id_type=MESH)

    for k in range(1, groups):
        pl.semaphore_signal(
            barrier, 1, device_id={"head": lax.rem(mine + k, groups)}, device_id_type=MESH
        )
    peers = jnp.where(me > 0, 1, 0) + jnp.where(me < size - 1, 1, 0) + (groups - 1)
    pl.semaphore_wait(barrier, peers)

    @pl.when(me == 0)
    def _():
        inbox[...] = jnp.zeros_like(inbox)

    def copy(c):
        return pltpu.make_async_remote_copy(
            src_ref=outbox.at[c],
            dst_ref=inbox.at[c],
            send_sem=send_sem.at[c],
            recv_sem=recv_sem.at[c],
            device_id={"seq": me + 1},
            device_id_type=MESH,
        )

    def place(owner, h):
        return pl.ds(pl.multiple_of(owner * width + h * HD, HD), HD)

    def rows_of(owner):
        return pl.ds(pl.multiple_of(owner * own_rows, CH), own_rows)

    def hand_over(h, k):
        to = lax.rem(mine + k, groups)
        return pltpu.make_async_remote_copy(
            src_ref=finished.at[h, rows_of(to), :],
            dst_ref=exchanged.at[:, place(mine, h)],
            send_sem=row_send.at[h, to],
            recv_sem=row_recv.at[h, mine],
            device_id={"head": to},
            device_id_type=MESH,
        )

    def take_over(h, k):
        source = lax.rem(mine + k, groups)
        return pltpu.make_async_remote_copy(
            src_ref=finished.at[h, rows_of(source), :],
            dst_ref=exchanged.at[:, place(source, h)],
            send_sem=row_send.at[h, source],
            recv_sem=row_recv.at[h, source],
            device_id={"head": source},
            device_id_type=MESH,
        )

    for h in range(local_heads):

        def pass_on(m, carry):
            c = h * M + m

            @pl.when(me > 0)
            def _():
                copy(c).wait_recv()

            arrived = inbox[c].astype(jnp.float32)
            current[m] = arrived

            @pl.when(me < size - 1)
            def _():
                outbox[c] = (prod_ref[c] * arrived + mem_ref[c]).astype(jnp.bfloat16)
                copy(c).start()

            return carry

        lax.fori_loop(0, M, pass_on, 0)
        cols = slice(h * HD, (h + 1) * HD)

        def block(b, carry):
            rows = pl.ds(pl.multiple_of(b * CH, CH), CH)
            at = (b * local_heads + h) * 2
            entering = (
                entry_ref[at] * current[chosen[at]] + entry_ref[at + 1] * current[chosen[at + 1]]
            ).astype(jnp.bfloat16)
            carried = jnp.dot(q_ref[rows, cols], entering, preferred_element_type=jnp.float32)
            total = att_ref[rows, cols] + growth_ref[rows, h : h + 1] * carried
            scale = lax.rsqrt(jnp.mean(total * total, axis=-1, keepdims=True) + 1e-06)
            finished[h, rows, :] = (total * scale * gain_ref[:, cols]).astype(jnp.bfloat16)
            return carry

        lax.fori_loop(0, blocks, block, 0, unroll=4)
        for k in range(1, groups):
            hand_over(h, k).start()
        exchanged[:, place(mine, h)] = finished[h, rows_of(mine), :]

    fetch.wait()
    half = local_heads // 2
    tile = out_ref.shape[1] // 4
    for part in range(2):
        for h in range(part * half, (part + 1) * half):
            for k in range(1, groups):
                take_over(h, k).wait_recv()

        def project(n, carry):
            columns = pl.ds(pl.multiple_of(n * tile, HD), tile)
            if part == 0:
                total = jnp.zeros((own_rows, tile), jnp.float32)
            else:
                total = partial[:, columns]
            for source in range(groups):
                begin = source * width + part * half * HD
                depth = slice(begin, begin + half * HD)
                total += jnp.dot(
                    exchanged[:, depth], w_ref[depth, columns], preferred_element_type=jnp.float32
                )
            if part == 0:
                partial[:, columns] = total
            else:
                out_ref[:, columns] = total.astype(jnp.bfloat16)
            return carry

        lax.fori_loop(0, 4, project, 0)

    @pl.when(me < size - 1)
    def _():
        def drain(c, carry):
            copy(c).wait_send()
            return carry

        lax.fori_loop(0, pieces, drain, 0)

    for h in range(local_heads):
        for k in range(1, groups):
            hand_over(h, k).wait_send()


def per_device(
    tokens, w_query, w_key, w_value, w_out, norm_gain, forget_rate, routing, memory_blend_share
):
    tok_rows = tokens.shape[0]
    width = w_query.shape[1]
    local_heads = width // HD
    num_blocks = tok_rows // CH
    groups = lax.axis_size("head")
    own_rows, model = tok_rows // groups, w_out.shape[1]
    pieces = local_heads * M
    whole_out = lax.all_gather(w_out, "head", axis=0, tiled=True)

    def project(weight):
        return jnp.dot(tokens, weight, preferred_element_type=jnp.float32).astype(jnp.bfloat16)

    key_raw, value_rows, query = project(w_key), project(w_value), project(w_query)
    chosen = routing.reshape(-1)
    smem = pl.BlockSpec(memory_space=SMEM)
    vmem = pl.BlockSpec(memory_space=VMEM)
    attended, memory, growth, entry, products = pl.pallas_call(
        local_kernel,
        out_shape=(
            jax.ShapeDtypeStruct((tok_rows, width), jnp.float32),
            jax.ShapeDtypeStruct((pieces, HD, HD), jnp.float32),
            jax.ShapeDtypeStruct((tok_rows, local_heads), jnp.float32),
            jax.ShapeDtypeStruct((num_blocks * local_heads * 2, 1, HD), jnp.float32),
            jax.ShapeDtypeStruct((pieces, 1, HD), jnp.float32),
        ),
        in_specs=[smem] * 2 + [vmem] * 4,
        out_specs=(vmem,) * 5,
        compiler_params=pltpu.CompilerParams(vmem_limit_bytes=LIMIT),
        name="local",
    )(chosen, memory_blend_share.reshape(-1), query, key_raw, value_rows, forget_rate)
    return pl.pallas_call(
        chain_kernel,
        out_shape=jax.ShapeDtypeStruct((own_rows, model), jnp.bfloat16),
        in_specs=[smem] + [vmem] * 7 + [pl.BlockSpec(memory_space=pl.ANY)],
        out_specs=vmem,
        scratch_shapes=[
            VMEM((pieces, HD, HD), jnp.bfloat16),
            VMEM((pieces, HD, HD), jnp.bfloat16),
            VMEM((M, HD, HD), jnp.float32),
            VMEM((local_heads, tok_rows, HD), jnp.bfloat16),
            VMEM((own_rows, groups * width), jnp.bfloat16),
            VMEM((own_rows, model), jnp.float32),
            VMEM((groups * width, model), jnp.bfloat16),
            pltpu.SemaphoreType.DMA,
            pltpu.SemaphoreType.DMA((pieces,)),
            pltpu.SemaphoreType.DMA((pieces,)),
            pltpu.SemaphoreType.DMA((local_heads, groups)),
            pltpu.SemaphoreType.DMA((local_heads, groups)),
        ],
        compiler_params=pltpu.CompilerParams(
            collective_id=0, has_side_effects=True, vmem_limit_bytes=LIMIT
        ),
        name="chain",
    )(chosen, entry, products, memory, query, growth, attended, norm_gain[None], whole_out)


def solution(mesh):
    placed = (
        P("seq", None),
        P(None, "head"),
        P(None, "head"),
        P(None, "head"),
        P("head", None),
        P("head"),
        P("seq", "head"),
        P("seq", "head", None),
        P("seq", "head", None),
    )
    return jax.shard_map(
        per_device, mesh=mesh, in_specs=placed, out_specs=P(("seq", "head"), None), check_vma=False
    )
```

time: 130 us -> 132 us (1.015)
  waiting for transfers between devices: 0.71 us -> 30.7 us
  blocking collectives: 21.2 us -> 0 us
  Pallas kernels: 59.3 us -> 70.1 us
  matrix products: 20.1 us -> 12.3 us
  other arithmetic: 6.64 us -> 0 us
  local copies, waits for them, and re-layouts: 8.48 us -> 4.98 us
    all_gather x1, waiting for transfers between devices: 0.01 us -> 30 us  [per_device(): whole_out = lax.all_gather(w_out, 'head', axis=0, tiled=True)]
    all_to_all x1 -> x0, blocking collectives: 21.2 us -> none  [per_device(): lax.all_to_all(normed, 'head', split_axis=0, concat_axis=1, tiled=True)]
    pallas_call x1, Pallas kernels: 45.2 us -> 53.9 us  [per_device(): pl.pallas_call(chain_kernel, out_shape=jax.ShapeDtypeStruct((own_rows, mo...]
    dot_general x1 -> x0, matrix products: 6.7 us -> none  [per_device(): result = jnp.dot(exchanged, whole_out, preferred_element_type=jnp.float32)]
    another operation x1 -> x0, other arithmetic: 6.33 us -> none  [per_device(): jnp.cumsum(-forget_rate.reshape(num_blocks, CH, local_heads), axis=1)]
    unnamed x16 -> x18, local copies, waits for them, and re-layouts: 0.38 us -> 3.67 us
    all_to_all x1 -> x0, local copies, waits for them, and re-layouts: 2.26 us -> none  [per_device(): lax.all_to_all(normed, 'head', split_axis=0, concat_axis=1, tiled=True)]
    pallas_call x1, Pallas kernels: 14.1 us -> 16.2 us  [per_device(): pl.pallas_call(local_kernel, out_shape=(jax.ShapeDtypeStruct((tok_rows, w...]
  transfers between devices with their start and end apart: 1 -> 1, of which waited for: 0 -> 1; matrix products, arithmetic and copies ran while one was open for 22% -> 11% of each run, Pallas kernels for 46% -> 12%
where the time goes in v2:
time: 132 us
  Pallas kernels  70.1 us (53%)
  waiting for transfers between devices  30.7 us (23%)
  between operations  13.4 us (10%)
  matrix products  12.3 us (9%)
  local copies, waits for them, and re-layouts  4.98 us (4%)
    pallas_call x1, Pallas kernels, per_device(): pl.pallas_call(chain_kernel, out_shape=jax.ShapeDtypeStruct((own_rows, mo...  53.9 us
    all_gather x1, waiting for transfers between devices, per_device(): whole_out = lax.all_gather(w_out, 'head', axis=0, tiled=True)  30 us
    pallas_call x1, Pallas kernels, per_device(): pl.pallas_call(local_kernel, out_shape=(jax.ShapeDtypeStruct((tok_rows, w...  16.2 us
    dot_general x3, matrix products, project(): jnp.dot(tokens, weight, preferred_element_type=jnp.float32)  12.3 us
    unnamed x18, local copies, waits for them, and re-layouts  3.67 us
  transfers between devices with their start and end apart: 1, of which 1 were waited for; matrix products, arithmetic and copies ran while one was open for 11% of the time, Pallas kernels for 12%

profile of v2, /device:TPU:29, one launch (start us, length us, event | category | flops | bytes accessed | tf_op | source)
XLA Modules:
  0.0 131.6 jit_solution(251545552367857912)
XLA Ops:
  6.5 0.0 copy-start
  6.5 0.0 copy-start.2
  6.5 0.0 copy-start.1
  6.5 0.0 copy-start.3
  6.5 0.0 all-gather.2.cloned.1.call-start
  6.6 0.7 all-gather.2.cloned.1.call-update
  7.3 0.1 copy-done.2
  7.4 0.1 copy.13
  7.5 0.7 reshape.6.chosen
  8.2 0.0 copy-done.1
  8.2 1.0 copy.15.rate_ref
  9.2 0.0 copy-done.3
  9.2 0.1 copy.14
  9.3 0.6 reshape.7.shares
  9.9 0.0 copy-done
  9.9 0.0 copy-start.4
  9.9 0.0 copy-start.5
  9.9 5.6 %convolution_convert_fusion.2.q_ref = bf16[1024,512]{1,0:T(8,128)(2,1)} fusion(bf16[1024,2048]{1,0:T(8,128)(2,1)} %param.9, bf16[2048,512]{1,0:T(8,128)(2,1)S(1)} %copy-done), kind=kOutput, calls=%fused_computation.2 | convolution fusion | flops 2148007936 | bytes 7340032 | tf_op jit(solution)/shard_map/dot_general | solution.py:274
  15.6 0.0 copy-done.4
  15.6 0.0 copy-done.5
  15.6 0.0 copy-start.6
  15.6 3.3 %convolution_convert_fusion.v_ref = bf16[1024,512]{1,0:T(8,128)(2,1)} fusion(bf16[1024,2048]{1,0:T(8,128)(2,1)S(1)} %copy-done.4, bf16[2048,512]{1,0:T(8,128)(2,1)S(1)} %copy-done.5), kind=kOutput, calls=%fused_computation | convolution fusion | flops 2148007936 | bytes 7340032 | tf_op jit(solution)/shard_map/dot_general | solution.py:274
  18.9 0.0 copy-done.6
  18.9 3.4 %convolution_convert_fusion.1.k_ref = bf16[1024,512]{1,0:T(8,128)(2,1)} fusion(bf16[1024,2048]{1,0:T(8,128)(2,1)S(1)} %copy-done.4, bf16[2048,512]{1,0:T(8,128)(2,1)S(1)} %copy-done.6), kind=kOutput, calls=%fused_computation.1 | convolution fusion | flops 2148007936 | bytes 7340032 | tf_op jit(solution)/shard_map/dot_general | solution.py:274
  22.3 16.2 %local.1 = (f32[1024,512]{1,0:T(8,128)}, f32[32,128,128]{2,1,0:T(8,128)}, f32[1024,4]{1,0:T(8,128)}, f32[128,1,128]{2,1,0:T(1,128)}, f32[32,1,128]{2,1,0:T(1,128)}) custom-call(s32[128]{0:T(128)} %reshape.6.chosen, f32[128]{0:T(128)} %reshape.7.shares, bf16[1024,512]{1,0:T(8,128)(2,1)} %convolution_convert_fusion.2.q_ref, ...), custom_call_target="tpu_custom_call" | custom-call | tf_op jit(solution)/shard_map/local/pallas_call | solution.py:280
  38.5 30.0 %all-gather.2.cloned.1.call-done.w_hbm = bf16[2048,2048]{1,0:T(8,128)(2,1)} async-done(((bf16[512,2048]{1,0:T(8,128)(2,1)}), bf16[2048,2048]{1,0:T(8,128)(2,1)}) %all-gather.2.cloned.1.call-update) | async-done | bytes 8388624 | tf_op jit(solution)/shard_map/all_gather | solution.py:271
  68.5 53.9 %chain.1 = bf16[256,2048]{1,0:T(8,128)(2,1)} custom-call(s32[128]{0:T(128)} %reshape.6.chosen, f32[128,1,128]{2,1,0:T(1,128)} %get-tuple-element.10.entry_ref, f32[32,1,128]{2,1,0:T(1,128)} %get-tuple-element.11.prod_ref, f32[32,128,128]{2,1,0:T(8,128)} %get-tuple-element.12.mem_ref, bf16[1024,512]{1,0:T(8,128)(2,1)} %convolution_convert_fusion.2.q_ref, ...), custom_call_target="tpu_custom_call" | custom-call | tf_op jit(solution)/shard_map/chain/pallas_call | solution.py:294
  122.4 2.3 %copy.17 = bf16[256,2048]{1,0:T(8,128)(2,1)} copy(bf16[256,2048]{1,0:T(8,128)(2,1)} %chain.1) | data formatting | bytes 2097152
Async XLA Ops:
  6.5 3.4 %copy-start = (bf16[2048,512]{1,0:T(8,128)(2,1)S(1)}, bf16[2048,512]{1,0:T(8,128)(2,1)}, u32[]{:S(2)}) copy-start(bf16[2048,512]{1,0:T(8,128)(2,1)} %param.10) | copy-start | bytes 6291460
  6.5 0.8 copy-start.2
  6.5 1.6 %copy-start.1 = (f32[1024,4]{0,1:T(4,128)S(1)}, f32[1024,4]{0,1:T(4,128)}, u32[]{:S(2)}) copy-start(f32[1024,4]{0,1:T(4,128)} %param.15) | copy-start | bytes 49156
  6.5 2.6 %copy-start.3 = (f32[16,4,2]{0,2,1:T(2,128)S(1)}, f32[16,4,2]{0,2,1:T(2,128)}, u32[]{:S(2)}) copy-start(f32[16,4,2]{0,2,1:T(2,128)} %param.17) | copy-start | bytes 1540
  6.5 62.0 %all-gather.2.cloned.1.call-start = ((), (), s32[]{:S(2)}) async-start(), calls=%async_computation | async-start | bytes 10485760 | tf_op jit(solution)/shard_map/all_gather | solution.py:271
  9.9 5.6 %copy-start.4 = (bf16[1024,2048]{1,0:T(8,128)(2,1)S(1)}, bf16[1024,2048]{1,0:T(8,128)(2,1)}, u32[]{:S(2)}) copy-start(bf16[1024,2048]{1,0:T(8,128)(2,1)} %param.9) | copy-start | bytes 12582916
  9.9 5.6 %copy-start.5 = (bf16[2048,512]{1,0:T(8,128)(2,1)S(1)}, bf16[2048,512]{1,0:T(8,128)(2,1)}, u32[]{:S(2)}) copy-start(bf16[2048,512]{1,0:T(8,128)(2,1)} %param.12) | copy-start | bytes 6291460
  15.6 3.3 %copy-start.6 = (bf16[2048,512]{1,0:T(8,128)(2,1)S(1)}, bf16[2048,512]{1,0:T(8,128)(2,1)}, u32[]{:S(2)}) copy-start(bf16[2048,512]{1,0:T(8,128)(2,1)} %param.11) | copy-start | bytes 6291460
Sparse Core Ops, SparseCore 0:
  8.9 59.5 all-gather.1

commit v3 on v2

--- a/solution.py
+++ b/solution.py
@@ -95,16 +95,11 @@
     growth_ref,
     att_ref,
     gain_ref,
-    w_hbm,
-    out_ref,
+    exchanged,
     inbox,
     outbox,
     current,
     finished,
-    exchanged,
-    partial,
-    w_ref,
-    w_sem,
     send_sem,
     recv_sem,
     row_send,
@@ -117,8 +112,6 @@
     width = local_heads * HD
     blocks = q_ref.shape[0] // CH
     own_rows = q_ref.shape[0] // groups
-    fetch = pltpu.make_async_copy(w_hbm, w_ref, w_sem)
-    fetch.start()
     barrier = pltpu.get_barrier_semaphore()
 
     @pl.when(me > 0)
@@ -217,33 +210,9 @@
             hand_over(h, k).start()
         exchanged[:, place(mine, h)] = finished[h, rows_of(mine), :]
 
-    fetch.wait()
-    half = local_heads // 2
-    tile = out_ref.shape[1] // 4
-    for part in range(2):
-        for h in range(part * half, (part + 1) * half):
-            for k in range(1, groups):
-                take_over(h, k).wait_recv()
-
-        def project(n, carry):
-            columns = pl.ds(pl.multiple_of(n * tile, HD), tile)
-            if part == 0:
-                total = jnp.zeros((own_rows, tile), jnp.float32)
-            else:
-                total = partial[:, columns]
-            for source in range(groups):
-                begin = source * width + part * half * HD
-                depth = slice(begin, begin + half * HD)
-                total += jnp.dot(
-                    exchanged[:, depth], w_ref[depth, columns], preferred_element_type=jnp.float32
-                )
-            if part == 0:
-                partial[:, columns] = total
-            else:
-                out_ref[:, columns] = total.astype(jnp.bfloat16)
-            return carry
-
-        lax.fori_loop(0, 4, project, 0)
+    for h in range(local_heads):
+        for k in range(1, groups):
+            take_over(h, k).wait_recv()
 
     @pl.when(me < size - 1)
     def _():
@@ -266,7 +235,7 @@
     local_heads = width // HD
     num_blocks = tok_rows // CH
     groups = lax.axis_size("head")
-    own_rows, model = tok_rows // groups, w_out.shape[1]
+    own_rows = tok_rows // groups
     pieces = local_heads * M
     whole_out = lax.all_gather(w_out, "head", axis=0, tiled=True)
 
@@ -291,20 +260,16 @@
         compiler_params=pltpu.CompilerParams(vmem_limit_bytes=LIMIT),
         name="local",
     )(chosen, memory_blend_share.reshape(-1), query, key_raw, value_rows, forget_rate)
-    return pl.pallas_call(
+    exchanged = pl.pallas_call(
         chain_kernel,
-        out_shape=jax.ShapeDtypeStruct((own_rows, model), jnp.bfloat16),
-        in_specs=[smem] + [vmem] * 7 + [pl.BlockSpec(memory_space=pl.ANY)],
+        out_shape=jax.ShapeDtypeStruct((own_rows, groups * width), jnp.bfloat16),
+        in_specs=[smem] + [vmem] * 7,
         out_specs=vmem,
         scratch_shapes=[
             VMEM((pieces, HD, HD), jnp.bfloat16),
             VMEM((pieces, HD, HD), jnp.bfloat16),
             VMEM((M, HD, HD), jnp.float32),
             VMEM((local_heads, tok_rows, HD), jnp.bfloat16),
-            VMEM((own_rows, groups * width), jnp.bfloat16),
-            VMEM((own_rows, model), jnp.float32),
-            VMEM((groups * width, model), jnp.bfloat16),
-            pltpu.SemaphoreType.DMA,
             pltpu.SemaphoreType.DMA((pieces,)),
             pltpu.SemaphoreType.DMA((pieces,)),
             pltpu.SemaphoreType.DMA((local_heads, groups)),
@@ -314,7 +279,9 @@
             collective_id=0, has_side_effects=True, vmem_limit_bytes=LIMIT
         ),
         name="chain",
-    )(chosen, entry, products, memory, query, growth, attended, norm_gain[None], whole_out)
+    )(chosen, entry, products, memory, query, growth, attended, norm_gain[None])
+    result = jnp.dot(exchanged, whole_out, preferred_element_type=jnp.float32)
+    return result.astype(jnp.bfloat16)
 
 
 def solution(mesh):

time: 132 us -> 106 us (0.80)
  waiting for transfers between devices: 30.7 us -> 0.7 us
  matrix products: 12.3 us -> 19.4 us
  local copies, waits for them, and re-layouts: 4.98 us -> 2.67 us
    all_gather x1, waiting for transfers between devices: 30 us -> 0.02 us  [per_device(): whole_out = lax.all_gather(w_out, 'head', axis=0, tiled=True)]
    dot_general x0 -> x1, matrix products: none -> 7.02 us  [per_device(): result = jnp.dot(exchanged, whole_out, preferred_element_type=jnp.float32)]
    unnamed x18 -> x17, local copies, waits for them, and re-layouts: 3.67 us -> 1.37 us
  transfers between devices with their start and end apart: 1 -> 1, of which waited for: 1 -> 0; matrix products, arithmetic and copies ran while one was open for 11% -> 14% of each run, Pallas kernels for 12% -> 66%
where the time goes in v3:
time: 106 us
  Pallas kernels  69.4 us (65%)
  matrix products  19.4 us (18%)
  between operations  13.4 us (13%)
  local copies, waits for them, and re-layouts  2.67 us (3%)
    pallas_call x1, Pallas kernels, per_device(): pl.pallas_call(chain_kernel, out_shape=jax.ShapeDtypeStruct((own_rows, gr...  53.2 us
    pallas_call x1, Pallas kernels, per_device(): pl.pallas_call(local_kernel, out_shape=(jax.ShapeDtypeStruct((tok_rows, w...  16.2 us
    dot_general x3, matrix products, project(): jnp.dot(tokens, weight, preferred_element_type=jnp.float32)  12.3 us
    dot_general x1, matrix products, per_device(): result = jnp.dot(exchanged, whole_out, preferred_element_type=jnp.float32)  7.02 us
  transfers between devices with their start and end apart: 1, of which 0 were waited for; matrix products, arithmetic and copies ran while one was open for 14% of the time, Pallas kernels for 66%

profile of v3, /device:TPU:29, one launch (start us, length us, event | category | flops | bytes accessed | tf_op | source)
XLA Modules:
  0.0 105.6 jit_solution(17742617908612984165)
XLA Ops:
  6.5 0.0 copy-start
  6.5 0.0 copy-start.2
  6.5 0.0 copy-start.1
  6.5 0.0 copy-start.3
  6.5 0.0 all-gather.2.cloned.1.call-start
  6.6 0.7 all-gather.2.cloned.1.call-update
  7.3 0.1 copy-done.2
  7.4 0.1 copy.13
  7.5 0.7 reshape.6.chosen
  8.2 0.0 copy-done.1
  8.2 1.0 copy.15.rate_ref
  9.2 0.0 copy-done.3
  9.2 0.1 copy.14
  9.3 0.6 reshape.7.shares
  9.9 0.0 copy-done
  9.9 0.0 copy-start.4
  9.9 0.0 copy-start.5
  9.9 5.6 %convolution_convert_fusion.3.q_ref = bf16[1024,512]{1,0:T(8,128)(2,1)} fusion(bf16[1024,2048]{1,0:T(8,128)(2,1)} %param.9, bf16[2048,512]{1,0:T(8,128)(2,1)S(1)} %copy-done), kind=kOutput, calls=%fused_computation.3 | convolution fusion | flops 2148007936 | bytes 7340032 | tf_op jit(solution)/shard_map/dot_general | solution.py:243
  15.6 0.0 copy-done.4
  15.6 0.0 copy-done.5
  15.6 0.0 copy-start.6
  15.6 3.3 %convolution_convert_fusion.1.v_ref = bf16[1024,512]{1,0:T(8,128)(2,1)} fusion(bf16[1024,2048]{1,0:T(8,128)(2,1)S(1)} %copy-done.4, bf16[2048,512]{1,0:T(8,128)(2,1)S(1)} %copy-done.5), kind=kOutput, calls=%fused_computation.1 | convolution fusion | flops 2148007936 | bytes 7340032 | tf_op jit(solution)/shard_map/dot_general | solution.py:243
  18.9 0.0 copy-done.6
  18.9 3.4 %convolution_convert_fusion.2.k_ref = bf16[1024,512]{1,0:T(8,128)(2,1)} fusion(bf16[1024,2048]{1,0:T(8,128)(2,1)S(1)} %copy-done.4, bf16[2048,512]{1,0:T(8,128)(2,1)S(1)} %copy-done.6), kind=kOutput, calls=%fused_computation.2 | convolution fusion | flops 2148007936 | bytes 7340032 | tf_op jit(solution)/shard_map/dot_general | solution.py:243
  22.3 16.2 %local.1 = (f32[1024,512]{1,0:T(8,128)}, f32[32,128,128]{2,1,0:T(8,128)}, f32[1024,4]{1,0:T(8,128)}, f32[128,1,128]{2,1,0:T(1,128)}, f32[32,1,128]{2,1,0:T(1,128)}) custom-call(s32[128]{0:T(128)} %reshape.6.chosen, f32[128]{0:T(128)} %reshape.7.shares, bf16[1024,512]{1,0:T(8,128)(2,1)} %convolution_convert_fusion.3.q_ref, ...), custom_call_target="tpu_custom_call" | custom-call | tf_op jit(solution)/shard_map/local/pallas_call | solution.py:249
  38.5 53.2 %chain.1 = bf16[256,2048]{1,0:T(8,128)(2,1)} custom-call(s32[128]{0:T(128)} %reshape.6.chosen, f32[128,1,128]{2,1,0:T(1,128)} %get-tuple-element.10.entry_ref, f32[32,1,128]{2,1,0:T(1,128)} %get-tuple-element.11.prod_ref, f32[32,128,128]{2,1,0:T(8,128)} %get-tuple-element.12.mem_ref, bf16[1024,512]{1,0:T(8,128)(2,1)} %convolution_convert_fusion.3.q_ref, ...), custom_call_target="tpu_custom_call" | custom-call | tf_op jit(solution)/shard_map/chain/pallas_call | solution.py:263
  91.7 0.0 all-gather.2.cloned.1.call-done
  91.7 7.0 %convolution_convert_fusion = bf16[256,2048]{1,0:T(8,128)(2,1)} fusion(bf16[256,2048]{1,0:T(8,128)(2,1)} %chain.1, bf16[2048,2048]{1,0:T(8,128)(2,1)} %all-gather.2.cloned.1.call-done), kind=kOutput, calls=%fused_computation | convolution fusion | flops 2148007936 | bytes 10485760 | tf_op jit(solution)/shard_map/dot_general | solution.py:283
Async XLA Ops:
  6.5 3.4 %copy-start = (bf16[2048,512]{1,0:T(8,128)(2,1)S(1)}, bf16[2048,512]{1,0:T(8,128)(2,1)}, u32[]{:S(2)}) copy-start(bf16[2048,512]{1,0:T(8,128)(2,1)} %param.10) | copy-start | bytes 6291460
  6.5 0.8 copy-start.2
  6.5 1.6 %copy-start.1 = (f32[1024,4]{0,1:T(4,128)S(1)}, f32[1024,4]{0,1:T(4,128)}, u32[]{:S(2)}) copy-start(f32[1024,4]{0,1:T(4,128)} %param.15) | copy-start | bytes 49156
  6.5 2.6 %copy-start.3 = (f32[16,4,2]{0,2,1:T(2,128)S(1)}, f32[16,4,2]{0,2,1:T(2,128)}, u32[]{:S(2)}) copy-start(f32[16,4,2]{0,2,1:T(2,128)} %param.17) | copy-start | bytes 1540
  6.5 85.1 %all-gather.2.cloned.1.call-start = ((), (), s32[]{:S(2)}) async-start(), calls=%async_computation | async-start | bytes 10485760 | tf_op jit(solution)/shard_map/all_gather | solution.py:240
  9.9 5.6 %copy-start.4 = (bf16[1024,2048]{1,0:T(8,128)(2,1)S(1)}, bf16[1024,2048]{1,0:T(8,128)(2,1)}, u32[]{:S(2)}) copy-start(bf16[1024,2048]{1,0:T(8,128)(2,1)} %param.9) | copy-start | bytes 12582916
  9.9 5.6 %copy-start.5 = (bf16[2048,512]{1,0:T(8,128)(2,1)S(1)}, bf16[2048,512]{1,0:T(8,128)(2,1)}, u32[]{:S(2)}) copy-start(bf16[2048,512]{1,0:T(8,128)(2,1)} %param.12) | copy-start | bytes 6291460
  15.6 3.3 %copy-start.6 = (bf16[2048,512]{1,0:T(8,128)(2,1)S(1)}, bf16[2048,512]{1,0:T(8,128)(2,1)}, u32[]{:S(2)}) copy-start(bf16[2048,512]{1,0:T(8,128)(2,1)} %param.11) | copy-start | bytes 6291460
Sparse Core Ops, SparseCore 0:
  8.9 59.5 all-gather.1

commit v4 on v3

--- a/solution.py
+++ b/solution.py
@@ -13,6 +13,7 @@
 MESH = pl.DeviceIdType.MESH
 VMEM = pltpu.VMEM
 SMEM = pltpu.SMEM
+PARTS = 4
 LIMIT = 60 * 1024 * 1024
 
 
@@ -86,6 +87,10 @@
     lax.fori_loop(0, blocks, block, 0)
 
 
+def weights_of(owner, depth):
+    return pl.ds(pl.multiple_of(owner * depth, depth), depth)
+
+
 def chain_kernel(
     chosen,
     entry_ref,
@@ -95,7 +100,9 @@
     growth_ref,
     att_ref,
     gain_ref,
+    w_ref,
     exchanged,
+    gathered,
     inbox,
     outbox,
     current,
@@ -104,6 +111,11 @@
     recv_sem,
     row_send,
     row_recv,
+    own_sem,
+    near_send,
+    near_recv,
+    pass_send,
+    pass_recv,
 ):
     size, me = lax.axis_size("seq"), lax.axis_index("seq")
     groups, mine = lax.axis_size("head"), lax.axis_index("head")
@@ -170,6 +182,43 @@
             device_id={"head": source},
             device_id_type=MESH,
         )
+
+    twin = mine + 1 - 2 * lax.rem(mine, 2)
+    depth = w_ref.shape[0]
+    piece = depth // PARTS
+
+    def weights(owner, part):
+        return pl.ds(pl.multiple_of(owner * depth + part * piece, piece), piece)
+
+    def share(k, part):
+        to = twin if k == 0 else lax.rem(mine + 2 * k, groups)
+        return pltpu.make_async_remote_copy(
+            src_ref=w_ref.at[part * piece : (part + 1) * piece, :],
+            dst_ref=gathered.at[weights(mine, part), :],
+            send_sem=near_send.at[k, part],
+            recv_sem=near_recv.at[k, part],
+            device_id={"head": to},
+            device_id_type=MESH,
+        )
+
+    def relay(k, part):
+        source = lax.rem(mine + groups - 2 * k, groups)
+        return pltpu.make_async_remote_copy(
+            src_ref=gathered.at[weights(source, part), :],
+            dst_ref=gathered.at[weights(source, part), :],
+            send_sem=pass_send.at[k, part],
+            recv_sem=pass_recv.at[k, part],
+            device_id={"head": twin},
+            device_id_type=MESH,
+        )
+
+    keep = pltpu.make_async_copy(w_ref, gathered.at[weights_of(mine, depth), :], own_sem)
+    keep.start()
+    for part in range(PARTS):
+        for k in range(1, groups // 2):
+            share(k, part).start()
+    for part in range(PARTS):
+        share(0, part).start()
 
     for h in range(local_heads):
 
@@ -210,9 +259,23 @@
             hand_over(h, k).start()
         exchanged[:, place(mine, h)] = finished[h, rows_of(mine), :]
 
+    for part in range(PARTS):
+        for k in range(1, groups // 2):
+            share(k, part).wait_recv()
+            relay(k, part).start()
+
     for h in range(local_heads):
         for k in range(1, groups):
             take_over(h, k).wait_recv()
+
+    keep.wait()
+    for part in range(PARTS):
+        share(0, part).wait_recv()
+        for k in range(1, groups // 2):
+            relay(k, part).wait_recv()
+            relay(k, part).wait_send()
+        for k in range(groups // 2):
+            share(k, part).wait_send()
 
     @pl.when(me < size - 1)
     def _():
@@ -237,7 +300,6 @@
     groups = lax.axis_size("head")
     own_rows = tok_rows // groups
     pieces = local_heads * M
-    whole_out = lax.all_gather(w_out, "head", axis=0, tiled=True)
 
     def project(weight):
         return jnp.dot(tokens, weight, preferred_element_type=jnp.float32).astype(jnp.bfloat16)
@@ -260,11 +322,14 @@
         compiler_params=pltpu.CompilerParams(vmem_limit_bytes=LIMIT),
         name="local",
     )(chosen, memory_blend_share.reshape(-1), query, key_raw, value_rows, forget_rate)
-    exchanged = pl.pallas_call(
+    exchanged, whole_out = pl.pallas_call(
         chain_kernel,
-        out_shape=jax.ShapeDtypeStruct((own_rows, groups * width), jnp.bfloat16),
-        in_specs=[smem] + [vmem] * 7,
-        out_specs=vmem,
+        out_shape=(
+            jax.ShapeDtypeStruct((own_rows, groups * width), jnp.bfloat16),
+            jax.ShapeDtypeStruct((groups * w_out.shape[0], w_out.shape[1]), jnp.bfloat16),
+        ),
+        in_specs=[smem] + [vmem] * 8,
+        out_specs=(vmem, pl.BlockSpec(memory_space=pltpu.HBM)),
         scratch_shapes=[
             VMEM((pieces, HD, HD), jnp.bfloat16),
             VMEM((pieces, HD, HD), jnp.bfloat16),
@@ -274,12 +339,17 @@
             pltpu.SemaphoreType.DMA((pieces,)),
             pltpu.SemaphoreType.DMA((local_heads, groups)),
             pltpu.SemaphoreType.DMA((local_heads, groups)),
+            pltpu.SemaphoreType.DMA,
+            pltpu.SemaphoreType.DMA((groups // 2, PARTS)),
+            pltpu.SemaphoreType.DMA((groups // 2, PARTS)),
+            pltpu.SemaphoreType.DMA((groups // 2, PARTS)),
+            pltpu.SemaphoreType.DMA((groups // 2, PARTS)),
         ],
         compiler_params=pltpu.CompilerParams(
             collective_id=0, has_side_effects=True, vmem_limit_bytes=LIMIT
         ),
         name="chain",
-    )(chosen, entry, products, memory, query, growth, attended, norm_gain[None])
+    )(chosen, entry, products, memory, query, growth, attended, norm_gain[None], w_out)
     result = jnp.dot(exchanged, whole_out, preferred_element_type=jnp.float32)
     return result.astype(jnp.bfloat16)
 

time: 106 us -> 107 us (level); the launches traced: 106 us -> 105 us
  between operations: 13.4 us -> 0.02 us
  Pallas kernels: 69.4 us -> 80.8 us
  local copies, waits for them, and re-layouts: 2.67 us -> 4.96 us
    pallas_call x1, Pallas kernels: 53.2 us -> 64.8 us  [per_device(): pl.pallas_call(chain_kernel, out_shape=(jax.ShapeDtypeStruct((own_rows, g...]
    unnamed x17 -> x11, local copies, waits for them, and re-layouts: 1.37 us -> 3.5 us
  transfers between devices with their start and end apart: 1 -> 0, of which waited for: 0 -> 0; matrix products, arithmetic and copies ran while one was open for 14% -> 0% of each run, Pallas kernels for 66% -> 0%
where the time goes in v4:
time: 107 us; the launch traced here: 105 us
  Pallas kernels  80.8 us (76%)
  matrix products  19.3 us (18%)
  local copies, waits for them, and re-layouts  4.96 us (5%)
    pallas_call x1, Pallas kernels, per_device(): pl.pallas_call(chain_kernel, out_shape=(jax.ShapeDtypeStruct((own_rows, g...  64.8 us
    pallas_call x1, Pallas kernels, per_device(): pl.pallas_call(local_kernel, out_shape=(jax.ShapeDtypeStruct((tok_rows, w...  16 us
    dot_general x3, matrix products, project(): jnp.dot(tokens, weight, preferred_element_type=jnp.float32)  12.3 us
    dot_general x1, matrix products, per_device(): result = jnp.dot(exchanged, whole_out, preferred_element_type=jnp.float32)  7.02 us
    unnamed x11, local copies, waits for them, and re-layouts  3.5 us

profile of v4, /device:TPU:29, one launch (start us, length us, event | category | flops | bytes accessed | tf_op | source)
XLA Modules:
  0.0 105.1 jit_solution(4193383597757706927)
XLA Ops:
  0.0 0.0 copy-start
  0.0 0.9 copy.13
  0.9 0.7 reshape.6.chosen
  1.7 0.8 copy.14
  2.5 0.7 reshape.7.shares
  3.2 1.8 %copy.15.rate_ref = f32[1024,4]{1,0:T(8,128)} copy(f32[1024,4]{0,1:T(4,128)} %param.15) | data formatting | bytes 32768 | tf_op args[6]
  5.0 0.0 copy-done
  5.0 0.0 copy-start.1
  5.0 0.0 copy-start.2
  5.0 5.6 %convolution_convert_fusion.3.q_ref = bf16[1024,512]{1,0:T(8,128)(2,1)} fusion(bf16[1024,2048]{1,0:T(8,128)(2,1)} %param.9, bf16[2048,512]{1,0:T(8,128)(2,1)S(1)} %copy-done), kind=kOutput, calls=%fused_computation.3 | convolution fusion | flops 2148007936 | bytes 7340032 | tf_op jit(solution)/shard_map/dot_general | solution.py:305
  10.6 0.0 copy-done.1
  10.6 0.0 copy-done.2
  10.6 0.0 copy-start.3
  10.6 3.3 %convolution_convert_fusion.2.k_ref = bf16[1024,512]{1,0:T(8,128)(2,1)} fusion(bf16[1024,2048]{1,0:T(8,128)(2,1)S(1)} %copy-done.1, bf16[2048,512]{1,0:T(8,128)(2,1)S(1)} %copy-done.2), kind=kOutput, calls=%fused_computation.2 | convolution fusion | flops 2148007936 | bytes 7340032 | tf_op jit(solution)/shard_map/dot_general | solution.py:305
  13.9 0.0 copy-done.3
  13.9 3.3 %convolution_convert_fusion.1.v_ref = bf16[1024,512]{1,0:T(8,128)(2,1)} fusion(bf16[1024,2048]{1,0:T(8,128)(2,1)S(1)} %copy-done.1, bf16[2048,512]{1,0:T(8,128)(2,1)S(1)} %copy-done.3), kind=kOutput, calls=%fused_computation.1 | convolution fusion | flops 2148007936 | bytes 7340032 | tf_op jit(solution)/shard_map/dot_general | solution.py:305
  17.2 16.0 %local.1 = (f32[1024,512]{1,0:T(8,128)}, f32[32,128,128]{2,1,0:T(8,128)}, f32[1024,4]{1,0:T(8,128)}, f32[128,1,128]{2,1,0:T(1,128)}, f32[32,1,128]{2,1,0:T(1,128)}) custom-call(s32[128]{0:T(128)} %reshape.6.chosen, f32[128]{0:T(128)} %reshape.7.shares, bf16[1024,512]{1,0:T(8,128)(2,1)} %convolution_convert_fusion.3.q_ref, ...), custom_call_target="tpu_custom_call" | custom-call | tf_op jit(solution)/shard_map/local/pallas_call | solution.py:311
  33.3 64.8 %chain.1 = (bf16[256,2048]{1,0:T(8,128)(2,1)}, bf16[2048,2048]{1,0:T(8,128)(2,1)}) custom-call(s32[128]{0:T(128)} %reshape.6.chosen, f32[128,1,128]{2,1,0:T(1,128)} %get-tuple-element.12.entry_ref, f32[32,1,128]{2,1,0:T(1,128)} %get-tuple-element.13.prod_ref, f32[32,128,128]{2,1,0:T(8,128)} %get-tuple-element.14.mem_ref, ...), custom_call_target="tpu_custom_call" | custom-call | tf_op jit(solution)/shard_map/chain/pallas_call | solution.py:325
  98.1 7.0 %convolution_convert_fusion = bf16[256,2048]{1,0:T(8,128)(2,1)} fusion(bf16[256,2048]{1,0:T(8,128)(2,1)} %get-tuple-element.17, bf16[2048,2048]{1,0:T(8,128)(2,1)} %get-tuple-element.18), kind=kOutput, calls=%fused_computation | convolution fusion | flops 2148007936 | bytes 10485760 | tf_op jit(solution)/shard_map/dot_general | solution.py:353
Async XLA Ops:
  0.0 5.0 %copy-start = (bf16[2048,512]{1,0:T(8,128)(2,1)S(1)}, bf16[2048,512]{1,0:T(8,128)(2,1)}, u32[]{:S(2)}) copy-start(bf16[2048,512]{1,0:T(8,128)(2,1)} %param.10) | copy-start | bytes 6291460
  5.0 5.6 %copy-start.1 = (bf16[1024,2048]{1,0:T(8,128)(2,1)S(1)}, bf16[1024,2048]{1,0:T(8,128)(2,1)}, u32[]{:S(2)}) copy-start(bf16[1024,2048]{1,0:T(8,128)(2,1)} %param.9) | copy-start | bytes 12582916
  5.0 5.6 %copy-start.2 = (bf16[2048,512]{1,0:T(8,128)(2,1)S(1)}, bf16[2048,512]{1,0:T(8,128)(2,1)}, u32[]{:S(2)}) copy-start(bf16[2048,512]{1,0:T(8,128)(2,1)} %param.11) | copy-start | bytes 6291460
  10.6 3.3 %copy-start.3 = (bf16[2048,512]{1,0:T(8,128)(2,1)S(1)}, bf16[2048,512]{1,0:T(8,128)(2,1)}, u32[]{:S(2)}) copy-start(bf16[2048,512]{1,0:T(8,128)(2,1)} %param.12) | copy-start | bytes 6291460

commit v5 on v4

--- a/solution.py
+++ b/solution.py
@@ -18,7 +18,18 @@
 
 
 def local_kernel(
-    chosen, shares, q_ref, k_ref, v_ref, rate_ref, att_ref, mem_ref, growth_ref, entry_ref, prod_ref
+    chosen,
+    shares,
+    k_ref,
+    v_ref,
+    rate_ref,
+    key_ref,
+    state_ref,
+    mem_ref,
+    column_ref,
+    line_ref,
+    entry_ref,
+    prod_ref,
 ):
     tok_rows, local_heads = rate_ref.shape
     blocks = tok_rows // CH
@@ -26,7 +37,6 @@
     prod_ref[...] = jnp.ones_like(prod_ref)
     t = lax.broadcasted_iota(jnp.int32, (CH, CH), 0)
     s = lax.broadcasted_iota(jnp.int32, (CH, CH), 1)
-    causal = t >= s
 
     def block(b, carry):
         rows = pl.ds(pl.multiple_of(b * CH, CH), CH)
@@ -42,23 +52,16 @@
             preferred_element_type=jnp.float32,
         )
         growths = jnp.exp(columns)
-        growth_ref[rows, :] = growths
+        column_ref[rows, :] = columns
+        line_ref[b] = lines
         for h in range(local_heads):
             cols = slice(h * HD, (h + 1) * HD)
-            query = q_ref[rows, cols]
             wide = k_ref[rows, cols].astype(jnp.float32)
             values = v_ref[rows, cols]
             keys = wide * lax.rsqrt(jnp.sum(wide * wide, axis=-1, keepdims=True) + 1e-06)
             keys = keys.astype(jnp.bfloat16)
+            key_ref[rows, cols] = keys
             column = columns[:, h : h + 1]
-            line = lines[h : h + 1, :]
-            gaps = jnp.where(causal, column - line, 0.0)
-            decays = jnp.where(causal, jnp.exp(gaps), 0.0)
-            scores = lax.dot_general(
-                query, keys, (((1,), (1,)), ((), ())), preferred_element_type=jnp.float32
-            )
-            weighted = (scores * decays).astype(jnp.bfloat16)
-            within = jnp.dot(weighted, values, preferred_element_type=jnp.float32)
             ending = column[CH - 1 : CH]
             scaled = (keys.astype(jnp.float32) * jnp.exp(ending - column)).astype(jnp.bfloat16)
             written = lax.dot_general(
@@ -70,11 +73,7 @@
             fade = jnp.broadcast_to(growths[CH - 1 : CH, h : h + 1], (1, HD))
             old_a = mem_ref[first]
             old_b = mem_ref[second]
-            mixed = (share_a * old_a + share_b * old_b).astype(jnp.bfloat16)
-            carried = jnp.dot(query, mixed, preferred_element_type=jnp.float32)
-            att_ref[rows, cols] = (
-                growths[:, h : h + 1] * carried + (share_a + share_b) * within
-            )
+            state_ref[b * local_heads + h] = (share_a * old_a + share_b * old_b).astype(jnp.bfloat16)
             mem_ref[first] = fade * old_a + written
             mem_ref[second] = fade * old_b + written
             prod_a, prod_b = prod_ref[first], prod_ref[second]
@@ -93,12 +92,16 @@
 
 def chain_kernel(
     chosen,
+    shares,
     entry_ref,
     prod_ref,
     mem_ref,
     q_ref,
-    growth_ref,
-    att_ref,
+    key_ref,
+    v_ref,
+    column_ref,
+    line_ref,
+    state_ref,
     gain_ref,
     w_ref,
     exchanged,
@@ -183,6 +186,9 @@
             device_id_type=MESH,
         )
 
+    t = lax.broadcasted_iota(jnp.int32, (CH, CH), 0)
+    s = lax.broadcasted_iota(jnp.int32, (CH, CH), 1)
+    causal = t >= s
     twin = mine + 1 - 2 * lax.rem(mine, 2)
     depth = w_ref.shape[0]
     piece = depth // PARTS
@@ -246,10 +252,22 @@
             rows = pl.ds(pl.multiple_of(b * CH, CH), CH)
             at = (b * local_heads + h) * 2
             entering = (
-                entry_ref[at] * current[chosen[at]] + entry_ref[at + 1] * current[chosen[at + 1]]
+                state_ref[b * local_heads + h].astype(jnp.float32)
+                + entry_ref[at] * current[chosen[at]]
+                + entry_ref[at + 1] * current[chosen[at + 1]]
             ).astype(jnp.bfloat16)
-            carried = jnp.dot(q_ref[rows, cols], entering, preferred_element_type=jnp.float32)
-            total = att_ref[rows, cols] + growth_ref[rows, h : h + 1] * carried
+            query, keys, values = q_ref[rows, cols], key_ref[rows, cols], v_ref[rows, cols]
+            column = column_ref[rows, h : h + 1]
+            line = line_ref[b, h : h + 1, :]
+            gaps = jnp.where(causal, column - line, 0.0)
+            decays = jnp.where(causal, jnp.exp(gaps), 0.0)
+            scores = lax.dot_general(
+                query, keys, (((1,), (1,)), ((), ())), preferred_element_type=jnp.float32
+            )
+            weighted = (scores * decays).astype(jnp.bfloat16)
+            within = jnp.dot(weighted, values, preferred_element_type=jnp.float32)
+            carried = jnp.dot(query, entering, preferred_element_type=jnp.float32)
+            total = jnp.exp(column) * carried + (shares[at] + shares[at + 1]) * within
             scale = lax.rsqrt(jnp.mean(total * total, axis=-1, keepdims=True) + 1e-06)
             finished[h, rows, :] = (total * scale * gain_ref[:, cols]).astype(jnp.bfloat16)
             return carry
@@ -305,30 +323,32 @@
         return jnp.dot(tokens, weight, preferred_element_type=jnp.float32).astype(jnp.bfloat16)
 
     key_raw, value_rows, query = project(w_key), project(w_value), project(w_query)
-    chosen = routing.reshape(-1)
+    chosen, shares = routing.reshape(-1), memory_blend_share.reshape(-1)
     smem = pl.BlockSpec(memory_space=SMEM)
     vmem = pl.BlockSpec(memory_space=VMEM)
-    attended, memory, growth, entry, products = pl.pallas_call(
+    keys, states, memory, columns, lines, entry, products = pl.pallas_call(
         local_kernel,
         out_shape=(
-            jax.ShapeDtypeStruct((tok_rows, width), jnp.float32),
+            jax.ShapeDtypeStruct((tok_rows, width), jnp.bfloat16),
+            jax.ShapeDtypeStruct((num_blocks * local_heads, HD, HD), jnp.bfloat16),
             jax.ShapeDtypeStruct((pieces, HD, HD), jnp.float32),
             jax.ShapeDtypeStruct((tok_rows, local_heads), jnp.float32),
+            jax.ShapeDtypeStruct((num_blocks, local_heads, CH), jnp.float32),
             jax.ShapeDtypeStruct((num_blocks * local_heads * 2, 1, HD), jnp.float32),
             jax.ShapeDtypeStruct((pieces, 1, HD), jnp.float32),
         ),
-        in_specs=[smem] * 2 + [vmem] * 4,
-        out_specs=(vmem,) * 5,
+        in_specs=[smem] * 2 + [vmem] * 3,
+        out_specs=(vmem,) * 7,
         compiler_params=pltpu.CompilerParams(vmem_limit_bytes=LIMIT),
         name="local",
-    )(chosen, memory_blend_share.reshape(-1), query, key_raw, value_rows, forget_rate)
+    )(chosen, shares, key_raw, value_rows, forget_rate)
     exchanged, whole_out = pl.pallas_call(
         chain_kernel,
         out_shape=(
             jax.ShapeDtypeStruct((own_rows, groups * width), jnp.bfloat16),
             jax.ShapeDtypeStruct((groups * w_out.shape[0], w_out.shape[1]), jnp.bfloat16),
         ),
-        in_specs=[smem] + [vmem] * 8,
+        in_specs=[smem] * 2 + [vmem] * 11,
         out_specs=(vmem, pl.BlockSpec(memory_space=pltpu.HBM)),
         scratch_shapes=[
             VMEM((pieces, HD, HD), jnp.bfloat16),
@@ -349,7 +369,21 @@
             collective_id=0, has_side_effects=True, vmem_limit_bytes=LIMIT
         ),
         name="chain",
-    )(chosen, entry, products, memory, query, growth, attended, norm_gain[None], w_out)
+    )(
+        chosen,
+        shares,
+        entry,
+        products,
+        memory,
+        query,
+        keys,
+        value_rows,
+        columns,
+        lines,
+        states,
+        norm_gain[None],
+        w_out,
+    )
     result = jnp.dot(exchanged, whole_out, preferred_element_type=jnp.float32)
     return result.astype(jnp.bfloat16)
 

time: 107 us -> 105 us (0.981)
  Pallas kernels: 80.8 us -> 79.2 us
    pallas_call x1, Pallas kernels: 16 us -> 13.8 us  [per_device(): pl.pallas_call(local_kernel, out_shape=(jax.ShapeDtypeStruct((tok_rows, w...]
where the time goes in v5:
time: 105 us; the launch traced here: 103 us
  Pallas kernels  79.2 us (75%)
  matrix products  19.3 us (18%)
  local copies, waits for them, and re-layouts  4.79 us (5%)
    pallas_call x1, Pallas kernels, per_device(): pl.pallas_call(chain_kernel, out_shape=(jax.ShapeDtypeStruct((own_rows, g...  65.4 us
    pallas_call x1, Pallas kernels, per_device(): pl.pallas_call(local_kernel, out_shape=(jax.ShapeDtypeStruct((tok_rows, w...  13.8 us
    dot_general x3, matrix products, project(): jnp.dot(tokens, weight, preferred_element_type=jnp.float32)  12.3 us
    dot_general x1, matrix products, per_device(): result = jnp.dot(exchanged, whole_out, preferred_element_type=jnp.float32)  7.02 us
    unnamed x11, local copies, waits for them, and re-layouts  3.47 us

profile of v5, /device:TPU:29, one launch (start us, length us, event | category | flops | bytes accessed | tf_op | source)
XLA Modules:
  0.0 103.3 jit_solution(4873871769140164914)
XLA Ops:
  0.0 0.0 copy-start
  0.0 0.9 copy.13
  0.9 0.7 reshape.6.chosen
  1.6 0.8 copy.14
  2.4 0.6 reshape.7.shares
  3.1 1.7 %copy.15.rate_ref = f32[1024,4]{1,0:T(8,128)} copy(f32[1024,4]{0,1:T(4,128)} %param.15) | data formatting | bytes 32768 | tf_op args[6]
  4.8 0.0 copy-done
  4.8 0.0 copy-start.1
  4.8 0.0 copy-start.2
  4.8 5.7 %convolution_convert_fusion.2.v_ref = bf16[1024,512]{1,0:T(8,128)(2,1)} fusion(bf16[1024,2048]{1,0:T(8,128)(2,1)} %param.9, bf16[2048,512]{1,0:T(8,128)(2,1)S(1)} %copy-done), kind=kOutput, calls=%fused_computation.2 | convolution fusion | flops 2148007936 | bytes 7340032 | tf_op jit(solution)/shard_map/dot_general | solution.py:323
  10.5 0.0 copy-done.1
  10.5 0.0 copy-done.2
  10.5 0.0 copy-start.3
  10.5 3.3 %convolution_convert_fusion.1.q_ref = bf16[1024,512]{1,0:T(8,128)(2,1)} fusion(bf16[1024,2048]{1,0:T(8,128)(2,1)S(1)} %copy-done.1, bf16[2048,512]{1,0:T(8,128)(2,1)S(1)} %copy-done.2), kind=kOutput, calls=%fused_computation.1 | convolution fusion | flops 2148007936 | bytes 7340032 | tf_op jit(solution)/shard_map/dot_general | solution.py:323
  13.8 0.0 copy-done.3
  13.8 3.3 %convolution_convert_fusion.3.k_ref = bf16[1024,512]{1,0:T(8,128)(2,1)} fusion(bf16[1024,2048]{1,0:T(8,128)(2,1)S(1)} %copy-done.1, bf16[2048,512]{1,0:T(8,128)(2,1)S(1)} %copy-done.3), kind=kOutput, calls=%fused_computation.3 | convolution fusion | flops 2148007936 | bytes 7340032 | tf_op jit(solution)/shard_map/dot_general | solution.py:323
  17.1 13.8 %local.1 = (bf16[1024,512]{1,0:T(8,128)(2,1)}, bf16[64,128,128]{2,1,0:T(8,128)(2,1)}, f32[32,128,128]{2,1,0:T(8,128)}, f32[1024,4]{1,0:T(8,128)}, f32[16,4,64]{2...) custom-call(s32[128]{0:T(128)} %reshape.6.chosen, f32[128]{0:T(128)} %reshape.7.shares, ...), custom_call_target="tpu_custom_call" | custom-call | tf_op jit(solution)/shard_map/local/pallas_call | solution.py:329
  30.9 65.4 %chain.1 = (bf16[256,2048]{1,0:T(8,128)(2,1)}, bf16[2048,2048]{1,0:T(8,128)(2,1)}) custom-call(s32[128]{0:T(128)} %reshape.6.chosen, f32[128]{0:T(128)} %reshape.7.shares, f32[128,1,128]{2,1,0:T(1,128)} %get-tuple-element.14.entry_ref, f32[32,1,128]{2,1,0:T(1,128)} %get-tuple-element.15.prod_ref, f32[32,128,128]{2,1,0:T(8,128)} %get-tuple-element.16.mem_ref, ...), custom_call_target="tpu_custom_call" | custom-call | tf_op jit(solution)/shard_map/chain/pallas_call | solution.py:345
  96.3 7.0 %convolution_convert_fusion = bf16[256,2048]{1,0:T(8,128)(2,1)} fusion(bf16[256,2048]{1,0:T(8,128)(2,1)} %get-tuple-element.21, bf16[2048,2048]{1,0:T(8,128)(2,1)} %get-tuple-element.22), kind=kOutput, calls=%fused_computation | convolution fusion | flops 2148007936 | bytes 10485760 | tf_op jit(solution)/shard_map/dot_general | solution.py:387
Async XLA Ops:
  0.0 4.8 %copy-start = (bf16[2048,512]{1,0:T(8,128)(2,1)S(1)}, bf16[2048,512]{1,0:T(8,128)(2,1)}, u32[]{:S(2)}) copy-start(bf16[2048,512]{1,0:T(8,128)(2,1)} %param.12) | copy-start | bytes 6291460
  4.8 5.7 %copy-start.1 = (bf16[1024,2048]{1,0:T(8,128)(2,1)S(1)}, bf16[1024,2048]{1,0:T(8,128)(2,1)}, u32[]{:S(2)}) copy-start(bf16[1024,2048]{1,0:T(8,128)(2,1)} %param.9) | copy-start | bytes 12582916
  4.8 5.7 %copy-start.2 = (bf16[2048,512]{1,0:T(8,128)(2,1)S(1)}, bf16[2048,512]{1,0:T(8,128)(2,1)}, u32[]{:S(2)}) copy-start(bf16[2048,512]{1,0:T(8,128)(2,1)} %param.10) | copy-start | bytes 6291460
  10.5 3.3 %copy-start.3 = (bf16[2048,512]{1,0:T(8,128)(2,1)S(1)}, bf16[2048,512]{1,0:T(8,128)(2,1)}, u32[]{:S(2)}) copy-start(bf16[2048,512]{1,0:T(8,128)(2,1)} %param.11) | copy-start | bytes 6291460

commit v6 on v5

--- a/solution.py
+++ b/solution.py
@@ -83,7 +83,7 @@
             prod_ref[second] = fade * prod_b
         return carry
 
-    lax.fori_loop(0, blocks, block, 0)
+    lax.fori_loop(0, blocks, block, 0, unroll=4)
 
 
 def weights_of(owner, depth):

time: 105 us -> 103 us (0.981)
  Pallas kernels: 79.2 us -> 76.6 us
    pallas_call x1, Pallas kernels: 13.8 us -> 11.2 us  [per_device(): pl.pallas_call(local_kernel, out_shape=(jax.ShapeDtypeStruct((tok_rows, w...]
where the time goes in v6:
time: 103 us; the launch traced here: 101 us
  Pallas kernels  76.6 us (74%)
  matrix products  19.3 us (19%)
  local copies, waits for them, and re-layouts  4.79 us (5%)
    pallas_call x1, Pallas kernels, per_device(): pl.pallas_call(chain_kernel, out_shape=(jax.ShapeDtypeStruct((own_rows, g...  65.4 us
    dot_general x3, matrix products, project(): jnp.dot(tokens, weight, preferred_element_type=jnp.float32)  12.3 us
    pallas_call x1, Pallas kernels, per_device(): pl.pallas_call(local_kernel, out_shape=(jax.ShapeDtypeStruct((tok_rows, w...  11.2 us
    dot_general x1, matrix products, per_device(): result = jnp.dot(exchanged, whole_out, preferred_element_type=jnp.float32)  7.02 us
    unnamed x11, local copies, waits for them, and re-layouts  3.47 us

profile of v6, /device:TPU:29, one launch (start us, length us, event | category | flops | bytes accessed | tf_op | source)
XLA Modules:
  0.0 100.7 jit_solution(12652827400129761560)
XLA Ops:
  0.0 0.0 copy-start
  0.0 0.9 copy.13
  0.9 0.7 reshape.6.chosen
  1.6 0.8 copy.14
  2.4 0.6 reshape.7.shares
  3.1 1.7 %copy.15.rate_ref = f32[1024,4]{1,0:T(8,128)} copy(f32[1024,4]{0,1:T(4,128)} %param.15) | data formatting | bytes 32768 | tf_op args[6]
  4.8 0.0 copy-done
  4.8 0.0 copy-start.1
  4.8 0.0 copy-start.2
  4.8 5.7 %convolution_convert_fusion.2.v_ref = bf16[1024,512]{1,0:T(8,128)(2,1)} fusion(bf16[1024,2048]{1,0:T(8,128)(2,1)} %param.9, bf16[2048,512]{1,0:T(8,128)(2,1)S(1)} %copy-done), kind=kOutput, calls=%fused_computation.2 | convolution fusion | flops 2148007936 | bytes 7340032 | tf_op jit(solution)/shard_map/dot_general | solution.py:323
  10.5 0.0 copy-done.1
  10.5 0.0 copy-done.2
  10.5 0.0 copy-start.3
  10.5 3.3 %convolution_convert_fusion.1.q_ref = bf16[1024,512]{1,0:T(8,128)(2,1)} fusion(bf16[1024,2048]{1,0:T(8,128)(2,1)S(1)} %copy-done.1, bf16[2048,512]{1,0:T(8,128)(2,1)S(1)} %copy-done.2), kind=kOutput, calls=%fused_computation.1 | convolution fusion | flops 2148007936 | bytes 7340032 | tf_op jit(solution)/shard_map/dot_general | solution.py:323
  13.8 0.0 copy-done.3
  13.8 3.3 %convolution_convert_fusion.3.k_ref = bf16[1024,512]{1,0:T(8,128)(2,1)} fusion(bf16[1024,2048]{1,0:T(8,128)(2,1)S(1)} %copy-done.1, bf16[2048,512]{1,0:T(8,128)(2,1)S(1)} %copy-done.3), kind=kOutput, calls=%fused_computation.3 | convolution fusion | flops 2148007936 | bytes 7340032 | tf_op jit(solution)/shard_map/dot_general | solution.py:323
  17.1 11.2 %local.1 = (bf16[1024,512]{1,0:T(8,128)(2,1)}, bf16[64,128,128]{2,1,0:T(8,128)(2,1)}, f32[32,128,128]{2,1,0:T(8,128)}, f32[1024,4]{1,0:T(8,128)}, f32[16,4,64]{2...) custom-call(s32[128]{0:T(128)} %reshape.6.chosen, f32[128]{0:T(128)} %reshape.7.shares, ...), custom_call_target="tpu_custom_call" | custom-call | tf_op jit(solution)/shard_map/local/pallas_call | solution.py:329
  28.3 65.4 %chain.1 = (bf16[256,2048]{1,0:T(8,128)(2,1)}, bf16[2048,2048]{1,0:T(8,128)(2,1)}) custom-call(s32[128]{0:T(128)} %reshape.6.chosen, f32[128]{0:T(128)} %reshape.7.shares, f32[128,1,128]{2,1,0:T(1,128)} %get-tuple-element.14.entry_ref, f32[32,1,128]{2,1,0:T(1,128)} %get-tuple-element.15.prod_ref, f32[32,128,128]{2,1,0:T(8,128)} %get-tuple-element.16.mem_ref, ...), custom_call_target="tpu_custom_call" | custom-call | tf_op jit(solution)/shard_map/chain/pallas_call | solution.py:345
  93.7 7.0 %convolution_convert_fusion = bf16[256,2048]{1,0:T(8,128)(2,1)} fusion(bf16[256,2048]{1,0:T(8,128)(2,1)} %get-tuple-element.21, bf16[2048,2048]{1,0:T(8,128)(2,1)} %get-tuple-element.22), kind=kOutput, calls=%fused_computation | convolution fusion | flops 2148007936 | bytes 10485760 | tf_op jit(solution)/shard_map/dot_general | solution.py:387
Async XLA Ops:
  0.0 4.8 %copy-start = (bf16[2048,512]{1,0:T(8,128)(2,1)S(1)}, bf16[2048,512]{1,0:T(8,128)(2,1)}, u32[]{:S(2)}) copy-start(bf16[2048,512]{1,0:T(8,128)(2,1)} %param.12) | copy-start | bytes 6291460
  4.8 5.7 %copy-start.1 = (bf16[1024,2048]{1,0:T(8,128)(2,1)S(1)}, bf16[1024,2048]{1,0:T(8,128)(2,1)}, u32[]{:S(2)}) copy-start(bf16[1024,2048]{1,0:T(8,128)(2,1)} %param.9) | copy-start | bytes 12582916
  4.8 5.7 %copy-start.2 = (bf16[2048,512]{1,0:T(8,128)(2,1)S(1)}, bf16[2048,512]{1,0:T(8,128)(2,1)}, u32[]{:S(2)}) copy-start(bf16[2048,512]{1,0:T(8,128)(2,1)} %param.10) | copy-start | bytes 6291460
  10.5 3.3 %copy-start.3 = (bf16[2048,512]{1,0:T(8,128)(2,1)S(1)}, bf16[2048,512]{1,0:T(8,128)(2,1)}, u32[]{:S(2)}) copy-start(bf16[2048,512]{1,0:T(8,128)(2,1)} %param.11) | copy-start | bytes 6291460
